TPU v7x, 256 devices: a whole 4x4x8 slice. The times are simulated.
256 devices in a mesh: row: 32 (over x, y, z_hi), rep: 8 (over z_lo, core).
Axes of the slice: x: 4, y: 4, z: 8 (z_hi: 2, z_lo: 4; z = z_hi * 4 + z_lo), core: 2. Of those that a mesh axis runs over, the one named last changes fastest.
Arguments:
- features: bfloat16 [65536, 256], P(('row', 'rep')), may hold values from -24 to 24
- weight: bfloat16 [256, 256], replicated, may hold values from -2 to 2
- degrees: int32 [65536], P(('row', 'rep')), may hold values from 1 to 16416, as said below
- cotangent: bfloat16 [65536, 256], P(('row', 'rep')), may hold values from -6 to 6
- tile_cols: int32 [4096, 16], P(('row', 'rep')), may hold values from 0 to 63, as said below
- list_len: int32 [4096], P(('row', 'rep')), may hold values from 1 to 16, as said below
- tiles: bfloat16 [4096, 16, 128, 128], P(('row', 'rep')), may hold values from 0 to 1, as said below
Outputs:
- activated: bfloat16 [65536, 256], P(('row', 'rep'))
- grad_x: bfloat16 [65536, 256], P(('row', 'rep'))
- grad_w: float32 [256, 256], P('row')
Inputs may be any that keep to these rules, and one draw needn't show every extreme that they name: `tile_cols`: within one list the 16 column tiles are distinct. `list_len`: on every device some list has exactly 16 live slots. `tiles`: entries are 0 or 1. `degrees`: each node's degree exceeds the number of ones in its row of A; some node has exactly the largest value.
All inputs are finite; a program needn't handle non-finite values.
Results may differ from a plain program's by a relative error of at most 0.006.
Values may be sent and summed in bfloat16 or wider, within the bound.
No kernel may reach another device: no remote copies, remote signals or barrier semaphores. Data moves between devices by JAX's collectives and lax.ppermute only.
A program may use at most 128 MiB of HBM per device.

v0:
```python
import math

import jax
import jax.numpy as jnp
from jax import lax
from jax.sharding import PartitionSpec as P


def on_device(features, weight, degrees, cotangent, tile_cols, list_len, tiles):
    node_rows, feat_width = features.shape
    tile_rows = tiles.shape[0]
    slot_count = tiles.shape[1]
    tile_size = tiles.shape[2]
    inv_root = 1.0 / jnp.sqrt(degrees.astype(jnp.float32))
    scaled_feats = (features.astype(jnp.float32) * inv_root[:, None]).astype(jnp.bfloat16)
    gathered = lax.all_gather(scaled_feats, "row", axis=0, tiled=True)
    section_tiles = gathered.reshape(-1, tile_size, feat_width)
    live_slots = (jnp.arange(slot_count)[None, :] < list_len[:, None]).astype(jnp.bfloat16)
    pattern = tiles * live_slots[:, :, None, None]
    picked = section_tiles[tile_cols]
    partial_value = jnp.einsum(
        "tkab,tkbf->taf", pattern, picked, preferred_element_type=jnp.float32
    )
    partial_value = partial_value.reshape(tile_rows * tile_size, feat_width)
    summed = lax.psum_scatter(partial_value, "rep", scatter_dimension=0, tiled=True)
    pooled = (summed * inv_root[:, None]).astype(jnp.bfloat16)
    preact = jnp.dot(pooled, weight, preferred_element_type=jnp.float32)
    activated = jax.nn.silu(preact).astype(jnp.bfloat16)
    sigmoid_val = jax.nn.sigmoid(preact)
    grad_pre = (
        cotangent.astype(jnp.float32) * sigmoid_val * (1.0 + preact * (1.0 - sigmoid_val))
    ).astype(jnp.bfloat16)
    weight_local = lax.dot_general(
        pooled, grad_pre, (((0,), (0,)), ((), ())), preferred_element_type=jnp.float32
    )
    back_rows = lax.dot_general(
        grad_pre, weight, (((1,), (1,)), ((), ())), preferred_element_type=jnp.float32
    )
    back_rows = (back_rows * inv_root[:, None]).astype(jnp.bfloat16)
    back_block = lax.all_gather(back_rows, "rep", axis=0, tiled=True).reshape(
        tile_rows, tile_size, feat_width
    )
    col_tiles = section_tiles.shape[0]

    def add_row(running, step_inputs):
        row_pattern, row_cols, row_back = step_inputs
        contrib = jnp.einsum(
            "kab,af->kbf", row_pattern, row_back, preferred_element_type=jnp.float32
        )
        return (running.at[row_cols].add(contrib), None)

    zero_sums = jnp.zeros((col_tiles, tile_size, feat_width), jnp.float32)
    col_sums, _ = lax.scan(add_row, zero_sums, (pattern, tile_cols, back_block))
    reduced_cols = lax.psum_scatter(
        col_sums.reshape(-1, feat_width), "row", scatter_dimension=0, tiled=True
    )
    node_total = node_rows * lax.axis_size("row") * lax.axis_size("rep")
    weight_norm = 1.0 / math.sqrt(node_total)
    rows_each = feat_width // lax.axis_size("row")
    weight_all = lax.psum(weight_local, ("row", "rep"))
    weight_rows = lax.dynamic_slice_in_dim(
        weight_all, lax.axis_index("row") * rows_each, rows_each, 0
    )
    grad_x = (reduced_cols * inv_root[:, None]).astype(jnp.bfloat16)
    return (activated, grad_x, weight_rows * weight_norm)


def solution(mesh):
    return jax.shard_map(
        on_device,
        mesh=mesh,
        in_specs=(
            P(("row", "rep"), None),
            P(),
            P(("row", "rep")),
            P(("row", "rep"), None),
            P(("row", "rep"), None),
            P(("row", "rep")),
            P(("row", "rep"), None, None, None),
        ),
        out_specs=(P(("row", "rep"), None), P(("row", "rep"), None), P("row", None)),
        check_vma=False,
    )
```

profile of v0, /device:TPU:6, one launch (start us, length us, event | category | flops | bytes accessed | tf_op | source)
XLA Modules:
  0.0 870.1 jit_solution(6991699257325208380)
XLA Ops:
  7.9 1.7 multiply_convert_fusion.4
  10.5 12.3 %copy.10 = bf16[16,16,128,128]{2,3,1,0:T(8,128)(2,1)} copy(bf16[16,16,128,128]{3,2,1,0:T(8,128)(2,1)} %param.15) | data formatting | bytes 16777216 | tf_op args[6]
  22.9 7.2 broadcast_multiply_fusion
  30.1 94.9 %all-gather.3.cloned.1.call-done = bf16[8192,256]{1,0:T(8,128)(2,1)} async-done(((bf16[256,256]{1,0:T(8,128)(2,1)}), bf16[8192,256]{1,0:T(8,128)(2,1)}) %all-gather.3.cloned.1.call-update) | async-done | bytes 4194320 | tf_op jit(solution)/shard_map/all_gather | solution.py:16
  125.0 12.0 %gather_fusion = bf16[256,128,256]{2,1,0:T(8,128)(2,1)} fusion(bf16[64,128,256]{2,1,0:T(8,128)(2,1)} %bitcast.39, s32[1024]{0:T(1024)S(1)} %pad_clamp_fusion), kind=kCustom, calls=%fused_computation | custom fusion | bytes 33555456 | tf_op jit(solution)/shard_map/gather | solution.py:20
  137.0 12.5 %fusion.12 = f32[16,128,256,1]{2,1,3,0:T(8,128)} fusion(bf16[16,16,128,128]{2,3,1,0:T(8,128)(2,1)} %broadcast_multiply_fusion, bf16[16,16,128,256]{3,2,1,0:T(8,128)(2,1)} %bitcast.38), kind=kOutput, calls=%fused_computation.29 | convolution fusion | flops 2147483648 | bytes 27262976 | tf_op jit(solution)/shard_map/tkab,tkbf->taf/dot_general | solution.py:21
  149.6 36.9 %reduce-scatter.3.cloned.1.call-done = f32[256,256]{1,0:T(8,128)} async-done(((f32[2048,256]{1,0:T(8,128)}), f32[256,256]{1,0:T(8,128)}) %reduce-scatter.3.cloned.1.call-update) | async-done | bytes 262160 | tf_op jit(solution)/shard_map/reduce_scatter | solution.py:25
  186.6 1.9 multiply_convert_fusion.1
  189.4 2.0 fusion.10
  191.5 34.3 %all-gather.5.cloned.1.call-done = bf16[2048,256]{1,0:T(8,128)(2,1)} async-done(((bf16[256,256]{1,0:T(8,128)(2,1)}), bf16[2048,256]{1,0:T(8,128)(2,1)}) %all-gather.5.cloned.1.call-update) | async-done | bytes 1048592 | tf_op jit(solution)/shard_map/all_gather | solution.py:40
  225.8 4.3 broadcast_in_dim.5
  230.0 108.8 %while.10 = (s32[]{:T(128)}, f32[64,128,256]{2,1,0:T(8,128)}, s32[16,16]{1,0:T(8,128)}, bf16[16,16,128,128]{2,3,1,0:T(8,128)(2,1)}, bf16[16,128,256]{2,1,0:T(8,128)(2,1)}, /*index=5*/s32[]{:T(128)}) while((s32[]{:T(128)}, f32[64,128,256]{2,1,0:T(8,128)}, s32[16,16]{1,0:T(8,128)}, bf16[16,16,128,128]{2,3,1,0:T(8,128)(2,1)}, ...), condition=%wide.region_3.4_spmd, body=%wide.region_1.3_spmd.sunk | while | flops 134742064 | bytes 8979721 | solution.py:53
  232.2 4.6 scatter_fusion
  239.0 4.7 scatter_fusion
  245.8 4.6 scatter_fusion
  252.6 4.7 scatter_fusion
  259.5 4.6 scatter_fusion
  264.1 1.5 fusion.26
  266.3 4.7 scatter_fusion
  273.1 4.6 scatter_fusion
  279.9 4.6 scatter_fusion
  286.6 4.6 scatter_fusion
  293.4 4.6 scatter_fusion
  300.2 4.6 scatter_fusion
  307.0 4.7 scatter_fusion
  313.8 4.7 scatter_fusion
  320.6 4.7 scatter_fusion
  327.4 4.6 scatter_fusion
  334.2 4.6 scatter_fusion
  338.9 141.2 %all-reduce.2.cloned.1.call-done = f32[256,256]{1,0:T(8,128)} async-done(((f32[256,256]{1,0:T(8,128)}), f32[256,256]{1,0:T(8,128)}) %all-reduce.2.cloned.1.call-update) | async-done | bytes 262160 | tf_op jit(solution)/shard_map/psum | solution.py:60
  481.3 380.5 %reduce-scatter.5.cloned.1.call-done = f32[256,256]{1,0:T(8,128)} async-done(((f32[8192,256]{1,0:T(8,128)}), f32[256,256]{1,0:T(8,128)}) %reduce-scatter.5.cloned.1.call-update) | async-done | bytes 262160 | tf_op jit(solution)/shard_map/reduce_scatter | solution.py:54
  861.9 1.7 multiply_convert_fusion
  (54 shorter events, 37.1 us)
Async XLA Ops:
  7.2 179.4 %copy-start = (bf16[256,256]{1,0:T(8,128)(2,1)S(1)}, bf16[256,256]{1,0:T(8,128)(2,1)}, u32[]{:S(2)}) copy-start(bf16[256,256]{1,0:T(8,128)(2,1)} %param.10) | copy-start | bytes 393220
  7.2 117.9 %all-gather.3.cloned.1.call-start = ((), (), s32[]{:S(2)}) async-start(), calls=%async_computation.2 | async-start | bytes 4325376 | tf_op jit(solution)/shard_map/all_gather | solution.py:16
  9.6 176.9 %reduce-scatter.3.cloned.1.call-start = ((), (), s32[]{:S(2)}) async-start(), calls=%async_computation.3 | async-start | bytes 2359296 | tf_op jit(solution)/shard_map/reduce_scatter | solution.py:25
  10.5 12.4 %copy-start.1 = (s32[16]{0:T(128)S(1)}, s32[16]{0:T(128)}, u32[]{:S(2)}) copy-start(s32[16]{0:T(128)} %param.14) | copy-start | bytes 196
  137.0 49.6 %copy-start.2 = (bf16[256,256]{1,0:T(8,128)(2,1)S(1)}, bf16[256,256]{1,0:T(8,128)(2,1)}, u32[]{:S(2)}) copy-start(bf16[256,256]{1,0:T(8,128)(2,1)} %param.12) | copy-start | bytes 393220
  149.6 76.2 %all-gather.5.cloned.1.call-start = ((), (), s32[]{:S(2)}) async-start(), calls=%async_computation.4 | async-start | bytes 1179648 | tf_op jit(solution)/shard_map/all_gather | solution.py:40
  189.4 290.7 %all-reduce.2.cloned.1.call-start = ((), (), s32[]{:S(2)}) async-start(), calls=%async_computation.6 | async-start | bytes 524288 | tf_op jit(solution)/shard_map/psum | solution.py:60
  191.4 670.5 %reduce-scatter.5.cloned.1.call-start = ((), (), s32[]{:S(2)}) async-start(), calls=%async_computation.5 | async-start | bytes 8650752 | tf_op jit(solution)/shard_map/reduce_scatter | solution.py:54
Sparse Core Ops, SparseCore 0:
  12.0 112.9 all-gather.2
  149.7 36.8 reduce-scatter.2
  189.5 36.2 all-gather.4
  231.1 248.9 all-reduce.1
  482.4 379.3 reduce-scatter.4
where the time goes:
time: 872 us; the launch traced here: 870 us
  waiting for transfers between devices  688 us (79%)
  other arithmetic  98.8 us (11%)
  matrix products  40.6 us (5%)
  local copies, waits for them, and re-layouts  28.7 us (3%)
  between operations  13.8 us (2%)
    reduce_scatter x1, waiting for transfers between devices, on_device(): lax.psum_scatter(col_sums.reshape(-1, feat_width), 'row', scatter_dimensi...  381 us
    psum x1, waiting for transfers between devices, on_device(): weight_all = lax.psum(weight_local, ('row', 'rep'))  141 us
    all_gather x1, waiting for transfers between devices, on_device(): gathered = lax.all_gather(scaled_feats, 'row', axis=0, tiled=True)  94.9 us
    scatter-add x16, other arithmetic, add_row(): return (running.at[row_cols].add(contrib), None)  74.2 us
    reduce_scatter x1, waiting for transfers between devices, on_device(): lax.psum_scatter(partial_value, 'rep', scatter_dimension=0, tiled=True)  36.9 us
    all_gather x1, waiting for transfers between devices, on_device(): lax.all_gather(back_rows, 'rep', axis=0, tiled=True)  34.3 us
    dot_general x16, matrix products, add_row(): jnp.einsum('kab,af->kbf', row_pattern, row_back, preferred_element_type=j...  23.3 us
  transfers between devices with their start and end apart: 5, of which 5 were waited for; matrix products, arithmetic and copies ran while one was open for 16% of the time, Pallas kernels for 0%

commit v1 on v0

v1 whole, which is shorter than its diff:
```python
import functools
import math

import jax
import jax.numpy as jnp
from jax import lax
from jax.experimental import pallas as pl
from jax.experimental.pallas import tpu as pltpu
from jax.sharding import PartitionSpec as P

BF16 = jnp.bfloat16
F32 = jnp.float32
SIDE, DEPTH = 4, 2
RUN, CORES = 4, 2
SHIFTS = (1, 3, 2)
TILE = 128
EXTRA = 8


def slot_of(shift):
    return shift + (shift == 2).astype(jnp.int32) - (shift == 3).astype(jnp.int32)


def row_shift(value, move):
    pairs = []
    for x in range(SIDE):
        for y in range(SIDE):
            for z in range(DEPTH):
                to_x, to_y, to_z = move(x, y, z)
                pairs.append(
                    ((x * SIDE + y) * DEPTH + z, (to_x * SIDE + to_y) * DEPTH + to_z)
                )
    return lax.ppermute(value, "row", pairs)


def shift_x(value, step):
    return row_shift(value, lambda x, y, z: ((x + step) % SIDE, y, z))


def shift_y(value, step):
    return row_shift(value, lambda x, y, z: (x, (y + step) % SIDE, z))


def flip_z(value):
    return row_shift(value, lambda x, y, z: (x, y, 1 - z))


def shift_run(value, step):
    pairs = [
        (run * CORES + core, (run + step) % RUN * CORES + core)
        for run in range(RUN)
        for core in range(CORES)
    ]
    return lax.ppermute(value, "rep", pairs)


def flip_core(value):
    pairs = [
        (run * CORES + core, run * CORES + 1 - core)
        for run in range(RUN)
        for core in range(CORES)
    ]
    return lax.ppermute(value, "rep", pairs)


def total(parts):
    return functools.reduce(jnp.add, [part.astype(F32) for part in parts])


def gather_rows(own):
    first, second = own, flip_z(own)
    firsts = [first] + [shift_x(first, step) for step in SHIFTS]
    seconds = [second] + [shift_y(second, step) for step in SHIFTS]
    first, second = jnp.concatenate(firsts), jnp.concatenate(seconds)
    firsts = [first] + [shift_y(first, step) for step in SHIFTS]
    seconds = [second] + [shift_x(second, step) for step in SHIFTS]
    return firsts + seconds


def forward_kernel(lists, cols, lens, tiles, *refs):
    pieces, (out, feats, sems) = refs[:-3], refs[-3:]
    step = pl.program_id(0)
    per_piece = feats.shape[0] // len(pieces)

    @pl.when(step == 0)
    def _():
        copies = [
            pltpu.make_async_copy(
                piece, feats.at[pl.ds(i * per_piece, per_piece)], sems.at[i]
            )
            for i, piece in enumerate(pieces)
        ]
        for copy in copies:
            copy.start()
        for copy in copies:
            copy.wait()

    row = lists[step]
    live = lens[row]
    slots = tiles.shape[1]
    half = slots // 2

    def part(first):
        left = [
            jnp.where(k < live, tiles[0, k], jnp.zeros_like(tiles[0, k]))
            for k in range(first, first + half)
        ]
        right = [feats[cols[row * slots + k]] for k in range(first, first + half)]
        return jnp.dot(
            jnp.concatenate(left, axis=1),
            jnp.concatenate(right, axis=0),
            preferred_element_type=F32,
        )

    @pl.when(live <= half)
    def _():
        out[0] = part(0).astype(out.dtype)

    @pl.when(live > half)
    def _():
        out[0] = (part(0) + part(half)).astype(out.dtype)


def forward(tiles, lists, cols, lens, pieces):
    count, slots, side, _ = tiles.shape
    width = pieces[0].shape[-1]
    pieces = [piece.reshape(-1, side, width) for piece in pieces]
    held = sum(piece.shape[0] for piece in pieces)
    return pl.pallas_call(
        forward_kernel,
        name="forward_product",
        out_shape=jax.ShapeDtypeStruct((lists.shape[0], side, width), BF16),
        grid_spec=pltpu.PrefetchScalarGridSpec(
            num_scalar_prefetch=3,
            grid=(lists.shape[0],),
            in_specs=[
                pl.BlockSpec((1, slots, side, side), lambda s, t, c, n: (t[s], 0, 0, 0))
            ]
            + [pl.BlockSpec(memory_space=pl.ANY)] * len(pieces),
            out_specs=pl.BlockSpec((1, side, width), lambda s, t, c, n: (s, 0, 0)),
            scratch_shapes=[
                pltpu.VMEM((held, side, width), BF16),
                pltpu.SemaphoreType.DMA((len(pieces),)),
            ],
        ),
        cost_estimate=pl.CostEstimate(
            flops=2 * lists.shape[0] * slots * side * side * width,
            bytes_accessed=2 * (lists.shape[0] * slots * side * side + held * side * width),
            transcendentals=0,
        ),
    )(lists, cols, lens, tiles, *pieces)


def middle_kernel(own, one, two, three, inv, cot, weight, act, back, grad):
    summed = (
        own[...].astype(F32)
        + one[...].astype(F32)
        + two[...].astype(F32)
        + three[...].astype(F32)
    )
    pooled = (summed * inv[...]).astype(BF16)
    pre = jnp.dot(pooled, weight[...], preferred_element_type=F32)
    sig = jax.nn.sigmoid(pre)
    act[...] = (pre * sig).astype(BF16)
    grad_pre = (cot[...].astype(F32) * sig * (1.0 + pre * (1.0 - sig))).astype(BF16)
    rows = lax.dot_general(
        grad_pre, weight[...], (((1,), (1,)), ((), ())), preferred_element_type=F32
    )
    back[...] = (rows * inv[...]).astype(BF16)
    grad[...] = lax.dot_general(
        pooled, grad_pre, (((0,), (0,)), ((), ())), preferred_element_type=F32
    )


def middle(parts, inv, cotangent, weight):
    rows, width = cotangent.shape
    return pl.pallas_call(
        middle_kernel,
        name="dense_middle",
        out_shape=(
            jax.ShapeDtypeStruct((rows, width), BF16),
            jax.ShapeDtypeStruct((rows, width), BF16),
            jax.ShapeDtypeStruct((width, width), F32),
        ),
    )(*parts, inv, cotangent, weight)


def backward_kernel(chunks, cols, lens, tiles, near, far, grad, out_a, out_b, sums, rows):
    step = pl.program_id(0)
    last = pl.num_programs(0) - 1
    half = pl.num_programs(0) // 2

    @pl.when(step == 0)
    def _():
        sums[...] = jnp.zeros_like(sums)

    @pl.when(step < half)
    def _():
        rows[...] = near[0]

    @pl.when(step >= half)
    def _():
        rows[...] = far[0]

    row = chunks[step]
    live = lens[row]
    slots = tiles.shape[1]
    group = 4
    for first in range(0, slots, group):

        @pl.when(first < live)
        def _():
            for k in range(first, first + group):
                tile = jnp.where(k < live, tiles[0, k], jnp.zeros_like(tiles[0, k]))
                place = cols[row * slots + k]
                sums[place] += lax.dot_general(
                    tile, rows[...], (((0,), (0,)), ((), ())), preferred_element_type=F32
                )

    @pl.when(step == last)
    def _():
        count = SIDE * SIDE * DEPTH
        base = pl.num_programs(0)

        @pl.loop(0, count)
        def _(i):
            out_a[i, pl.ds(0, TILE), :] = sums[i].astype(BF16)
            out_b[i] = sums[count + i].astype(BF16)
            source = pl.multiple_of(chunks[base + i] * EXTRA, EXTRA)
            out_a[i, pl.ds(TILE, EXTRA), :] = grad[pl.ds(source, EXTRA), :].astype(BF16)


def backward(tiles, table, cols, lens, near, far, grad):
    count, slots, side, _ = tiles.shape
    width = grad.shape[-1]
    near, far = [part.reshape(-1, side, width) for part in (near, far)]
    half = count // 2
    chunks = SIDE * SIDE * DEPTH
    whole = lambda *shape: pl.BlockSpec(shape, lambda s, t, c, n: (0,) * len(shape))
    return pl.pallas_call(
        backward_kernel,
        name="backward_product",
        out_shape=(
            jax.ShapeDtypeStruct((chunks, side + EXTRA, width), BF16),
            jax.ShapeDtypeStruct((chunks, side, width), BF16),
        ),
        grid_spec=pltpu.PrefetchScalarGridSpec(
            num_scalar_prefetch=3,
            grid=(count,),
            in_specs=[
                pl.BlockSpec((1, slots, side, side), lambda s, t, c, n: (t[s], 0, 0, 0)),
                pl.BlockSpec(
                    (1, side, width), lambda s, t, c, n: (jnp.minimum(s, half - 1), 0, 0)
                ),
                pl.BlockSpec(
                    (1, side, width), lambda s, t, c, n: (jnp.maximum(s - half, 0), 0, 0)
                ),
                whole(width, width),
            ],
            out_specs=(
                whole(chunks, side + EXTRA, width),
                whole(chunks, side, width),
            ),
            scratch_shapes=[
                pltpu.VMEM((2 * chunks, side, width), F32),
                pltpu.VMEM((side, width), BF16),
            ],
        ),
        cost_estimate=pl.CostEstimate(
            flops=2 * count * slots * side * side * width,
            bytes_accessed=2 * (count * slots * side * side + 4 * chunks * side * width),
            transcendentals=0,
        ),
    )(table, cols, lens, tiles, near, far, grad)


def scatter_rows(first, second):
    rows_a, rows_b, width = TILE + EXTRA, TILE, first.shape[-1]
    first = first.reshape(SIDE, SIDE * DEPTH * rows_a, width)
    second = second.reshape(SIDE, SIDE * DEPTH * rows_b, width)
    firsts = [first[0]] + [shift_x(first[step], step) for step in SHIFTS]
    seconds = [second[0]] + [shift_y(second[step], step) for step in SHIFTS]
    first = total(firsts).astype(BF16).reshape(SIDE, DEPTH * rows_a, width)
    second = total(seconds).astype(BF16).reshape(SIDE, DEPTH * rows_b, width)
    firsts = [first[0]] + [shift_y(first[step], step) for step in SHIFTS]
    seconds = [second[0]] + [shift_x(second[step], step) for step in SHIFTS]
    first, second = total(firsts), total(seconds)
    away = jnp.concatenate([first[rows_a:], second[rows_b:]]).astype(BF16)
    keep = jnp.concatenate([first[:rows_a], second[:rows_b]])
    return keep + flip_z(away).astype(F32)


def on_device(features, weight, degrees, cotangent, tile_cols, list_len, tiles):
    node_rows, width = features.shape
    count, slots = tile_cols.shape
    row_id, rep_id = lax.axis_index("row"), lax.axis_index("rep")
    x, y, z = row_id // (SIDE * DEPTH), row_id // DEPTH % SIDE, row_id % DEPTH
    run, core = rep_id // CORES, rep_id % CORES

    inv_root = 1.0 / jnp.sqrt(degrees.astype(F32))
    scaled = (features.astype(F32) * inv_root[:, None]).astype(BF16)
    inv_wide = jnp.broadcast_to(inv_root[:, None], (node_rows, width))

    share, part = tile_cols // 2, tile_cols % 2
    col_x, col_y, col_z = share // (SIDE * DEPTH), share // DEPTH % SIDE, share % DEPTH
    other = (col_z != z).astype(jnp.int32)
    from_x, from_y = slot_of((x - col_x) % SIDE), slot_of((y - col_y) % SIDE)
    near = jnp.where(other == 0, from_y * SIDE + from_x, from_x * SIDE + from_y)
    gather_cols = ((other * SIDE * SIDE + near) * 2 + part).reshape(-1)
    to_x, to_y = (col_x - x) % SIDE, (col_y - y) % SIDE
    far = jnp.where(part == 0, to_x * SIDE + to_y, to_y * SIDE + to_x)
    scatter_cols = ((part * SIDE * SIDE + far) * DEPTH + other).reshape(-1)

    order = jnp.arange(count)
    order_core = jnp.where(order < count // 2, core, 1 - core)
    steps = order // 2 % RUN
    sent_run, got_run = (run + steps) % RUN, (run - steps) % RUN
    sent_lists = (sent_run * CORES + order_core) * 2 + order % 2
    met = jnp.where(steps == 2, 3, jnp.where(steps == 3, 2, steps))
    met_run = (run - met) % RUN
    got_lists = (met_run * CORES + order_core) * 2 + order % 2
    chunk = jnp.arange(SIDE * SIDE * DEPTH)
    chunk_x, chunk_y = chunk // (SIDE * DEPTH), chunk // DEPTH % SIDE
    chunk_z = jnp.where(chunk % DEPTH == 0, z, 1 - z)
    chunk_rows = ((x + chunk_x) % SIDE * SIDE + (y + chunk_y) % SIDE) * DEPTH + chunk_z
    table = jnp.concatenate([got_lists, chunk_rows])

    pieces = gather_rows(scaled)
    partial_rows = forward(tiles, sent_lists, gather_cols, list_len, pieces)
    partial_rows = partial_rows.reshape(CORES, RUN, node_rows, width)
    mine = total([partial_rows[0], flip_core(partial_rows[1])]).astype(BF16)
    parts = [mine[0]] + [shift_run(mine[step], step) for step in SHIFTS]
    activated, back_rows, weight_part = middle(parts, inv_wide, cotangent, weight)

    near_rows = jnp.concatenate(
        [back_rows] + [shift_run(back_rows, step) for step in SHIFTS]
    )
    far_rows = flip_core(near_rows)
    first, second = backward(
        tiles, table, scatter_cols, list_len, near_rows, far_rows, weight_part
    )
    kept = scatter_rows(first, second)

    sums = jnp.concatenate([kept[:TILE], kept[TILE + EXTRA :]])
    grad_x = (sums * inv_root[:, None]).astype(BF16)
    weight_rows = kept[TILE : TILE + EXTRA]
    weight_rows = weight_rows + flip_core(weight_rows)
    weight_rows = total([weight_rows] + [shift_run(weight_rows, step) for step in SHIFTS])
    node_total = node_rows * lax.axis_size("row") * lax.axis_size("rep")
    return activated, grad_x, weight_rows * (1.0 / math.sqrt(node_total))


def solution(mesh):
    return jax.shard_map(
        on_device,
        mesh=mesh,
        in_specs=(
            P(("row", "rep"), None),
            P(),
            P(("row", "rep")),
            P(("row", "rep"), None),
            P(("row", "rep"), None),
            P(("row", "rep")),
            P(("row", "rep"), None, None, None),
        ),
        out_specs=(P(("row", "rep"), None), P(("row", "rep"), None), P("row", None)),
        check_vma=False,
    )
```

time: 872 us -> 217 us (0.25)
  waiting for transfers between devices: 688 us -> 88.6 us
  other arithmetic: 98.8 us -> 5.26 us
  starting transfers between devices: 0.2 us -> 77.6 us
  matrix products: 40.6 us -> 0 us
  Pallas kernels: 0 us -> 33.6 us
  local copies, waits for them, and re-layouts: 28.7 us -> 7.98 us
  between operations: 13.8 us -> 0.97 us
    reduce_scatter x2 -> x0, waiting for transfers between devices: 417 us -> none  [the longest x1 381 us: on_device(): lax.psum_scatter(col_sums.reshape(-1, feat_width), 'row', scatter_dimensi...]
    psum x1 -> x0, waiting for transfers between devices: 141 us -> none  [on_device(): weight_all = lax.psum(weight_local, ('row', 'rep'))]
    all_gather x2 -> x0, waiting for transfers between devices: 129 us -> none  [the longest x1 94.9 us: on_device(): gathered = lax.all_gather(scaled_feats, 'row', axis=0, tiled=True)]
    ppermute x0 -> x38, waiting for transfers between devices: none -> 88.6 us  [the longest x26 61.8 us: row_shift(): return lax.ppermute(value, 'row', pairs)]
    ppermute x0 -> x38, starting transfers between devices: none -> 77.6 us  [the longest x26 65.4 us: row_shift(): return lax.ppermute(value, 'row', pairs)]
    scatter-add x16 -> x0, other arithmetic: 74.2 us -> none  [add_row(): return (running.at[row_cols].add(contrib), None)]
    dot_general x20 -> x0, matrix products: 40.6 us -> none  [the longest x16 23.3 us: add_row(): jnp.einsum('kab,af->kbf', row_pattern, row_back, preferred_element_type=j...]
    pallas_call x0 -> x3, Pallas kernels: none -> 33.6 us  [the longest x1 16.2 us: backward(): pl.pallas_call(backward_kernel, name='backward_product', out_shape=(jax.S...]
  transfers between devices with their start and end apart: 5 -> 38, of which waited for: 5 -> 25; matrix products, arithmetic and copies ran while one was open for 16% -> 2% of each run, Pallas kernels for 0% -> 0%
where the time goes in v1:
time: 217 us; the launch traced here: 214 us
  waiting for transfers between devices  88.6 us (41%)
  starting transfers between devices  77.6 us (36%)
  Pallas kernels  33.6 us (15%)
  local copies, waits for them, and re-layouts  7.98 us (4%)
  other arithmetic  5.26 us (2%)
    ppermute x26, starting transfers between devices, row_shift(): return lax.ppermute(value, 'row', pairs)  65.4 us
    ppermute x26, waiting for transfers between devices, row_shift(): return lax.ppermute(value, 'row', pairs)  61.8 us
    ppermute x9, waiting for transfers between devices, shift_run(): return lax.ppermute(value, 'rep', pairs)  23.2 us
    pallas_call x1, Pallas kernels, backward(): pl.pallas_call(backward_kernel, name='backward_product', out_shape=(jax.S...  16.2 us
    pallas_call x1, Pallas kernels, forward(): pl.pallas_call(forward_kernel, name='forward_product', out_shape=jax.Shap...  15 us
    ppermute x9, starting transfers between devices, shift_run(): return lax.ppermute(value, 'rep', pairs)  11.9 us
  transfers between devices with their start and end apart: 38, of which 25 were waited for; matrix products, arithmetic and copies ran while one was open for 2% of the time, Pallas kernels for 0%

profile of v1, /device:TPU:6, one launch (start us, length us, event | category | flops | bytes accessed | tf_op | source)
XLA Modules:
  0.0 214.1 jit_solution(6171434044691372121)
XLA Ops:
  7.1 7.2 %collective-permute-start.6 = (bf16[256,256]{1,0:T(8,128)(2,1)S(1)}, bf16[256,256]{1,0:T(8,128)(2,1)S(1)}, u32[]{:S(2)}, u32[]{:S(2)}) collective-permute-start(bf16[256,256]{1,0:T(8,128)(2,1)S(1)} %multiply_convert_fusion), channel_id=1, source_target_pairs={{0,8},{8,0},{16,24},{24,16},{32,40},{40,32},{48,56},{56,48},{64,72... | collective-permute-start | bytes 393224 | tf_op jit(solution)/shard_map/ppermute | solution.py:33
  16.0 2.7 %collective-permute-done.6 = bf16[256,256]{1,0:T(8,128)(2,1)S(1)} collective-permute-done((bf16[256,256]{1,0:T(8,128)(2,1)S(1)}, bf16[256,256]{1,0:T(8,128)(2,1)S(1)}, u32[]{:S(2)}, u32[]{:S(2)}) %collective-permute-start.6) | collective-permute-done | bytes 131104 | tf_op jit(solution)/shard_map/ppermute | solution.py:33
  21.9 2.0 collective-permute-start.5
  25.0 7.2 %collective-permute-done.7 = bf16[256,256]{1,0:T(8,128)(2,1)S(1)} collective-permute-done((bf16[256,256]{1,0:T(8,128)(2,1)S(1)}, bf16[256,256]{1,0:T(8,128)(2,1)S(1)}, u32[]{:S(2)}, u32[]{:S(2)}) %collective-permute-start.7) | collective-permute-done | bytes 131104 | tf_op jit(solution)/shard_map/ppermute | solution.py:33
  32.2 13.4 %collective-permute-start.9 = (bf16[256,256]{1,0:T(8,128)(2,1)S(1)}, bf16[256,256]{1,0:T(8,128)(2,1)S(1)}, u32[]{:S(2)}, u32[]{:S(2)}) collective-permute-start(bf16[256,256]{1,0:T(8,128)(2,1)S(1)} %collective-permute-done.6), channel_id=1, source_target_pairs={{0,32},{8,40},{16,48},{24,56},{32,0},{40,8},{48,16},{56,24},{64,96... | collective-permute-start | bytes 393224 | tf_op jit(solution)/shard_map/ppermute | solution.py:33
  46.1 2.5 %collective-permute-done.9 = bf16[256,256]{1,0:T(8,128)(2,1)S(1)} collective-permute-done((bf16[256,256]{1,0:T(8,128)(2,1)S(1)}, bf16[256,256]{1,0:T(8,128)(2,1)S(1)}, u32[]{:S(2)}, u32[]{:S(2)}) %collective-permute-start.9) | collective-permute-done | bytes 131104 | tf_op jit(solution)/shard_map/ppermute | solution.py:33
  52.8 10.7 %collective-permute-done.10 = bf16[1024,256]{1,0:T(8,128)(2,1)S(1)} collective-permute-done((bf16[1024,256]{1,0:T(8,128)(2,1)S(1)}, bf16[1024,256]{1,0:T(8,128)(2,1)S(1)}, u32[]{:S(2)}, u32[]{:S(2)}) %collective-permute-start.10) | collective-permute-done | bytes 524320 | tf_op jit(solution)/shard_map/ppermute | solution.py:33
  63.5 7.6 %collective-permute-done.11 = bf16[1024,256]{1,0:T(8,128)(2,1)} collective-permute-done((bf16[1024,256]{1,0:T(8,128)(2,1)S(1)}, bf16[1024,256]{1,0:T(8,128)(2,1)}, u32[]{:S(2)}, u32[]{:S(2)}) %collective-permute-start.11) | collective-permute-done | bytes 524320 | tf_op jit(solution)/shard_map/ppermute | solution.py:33
  71.2 15.0 %forward_product.1 = bf16[16,128,256]{2,1,0:T(8,128)(2,1)} custom-call(s32[16]{0:T(128)} %multiply_add_fusion.2.lists, s32[256]{0:T(256)} %reshape.90.cols, s32[16]{0:T(128)} %lens.3, bf16[16,16,128,128]{3,2,1,0:T(8,128)(2,1)} %tiles.3, bf16[8,128,256]{2,1,0:T(8,128)(2,1)} %bitcast.35, bf16[8,128,256]{2,1,0:T(8,128)(2,1)} %bitcast.42, ...), custom_call_target="tpu_custom_call" | custom-call | flops 2147483648 | bytes 12582912 | tf_op jit(solution)/shard_map/forward_product/pallas_call | solution.py:129
  87.6 1.9 collective-permute-done.13
  91.6 2.5 %collective-permute-start.15 = (bf16[256,256]{1,0:T(8,128)(2,1)S(1)}, bf16[256,256]{1,0:T(8,128)(2,1)S(1)}, u32[]{:S(2)}, u32[]{:S(2)}) collective-permute-start(bf16[256,256]{1,0:T(8,128)(2,1)S(1)} %get-tuple-element.30), channel_id=1, source_target_pairs={{0,6},{1,7},{2,0},{3,1},{4,2},{5,3},{6,4},{7,5},{8,14},{9,15},{10,... | collective-permute-start | bytes 393224 | tf_op jit(solution)/shard_map/ppermute | solution.py:54
  94.2 2.1 collective-permute-start.16
  96.3 2.2 %collective-permute-done.14.one = bf16[256,256]{1,0:T(8,128)(2,1)S(1)} collective-permute-done((bf16[256,256]{1,0:T(8,128)(2,1)S(1)}, bf16[256,256]{1,0:T(8,128)(2,1)S(1)}, u32[]{:S(2)}, u32[]{:S(2)}) %collective-permute-start.14) | collective-permute-done | bytes 131104 | tf_op jit(solution)/shard_map/ppermute | solution.py:54
  98.5 2.3 %collective-permute-done.15.two = bf16[256,256]{1,0:T(8,128)(2,1)S(1)} collective-permute-done((bf16[256,256]{1,0:T(8,128)(2,1)S(1)}, bf16[256,256]{1,0:T(8,128)(2,1)S(1)}, u32[]{:S(2)}, u32[]{:S(2)}) %collective-permute-start.15) | collective-permute-done | bytes 131104 | tf_op jit(solution)/shard_map/ppermute | solution.py:54
  100.8 5.6 %collective-permute-done.16.three = bf16[256,256]{1,0:T(8,128)(2,1)S(1)} collective-permute-done((bf16[256,256]{1,0:T(8,128)(2,1)S(1)}, bf16[256,256]{1,0:T(8,128)(2,1)S(1)}, u32[]{:S(2)}, u32[]{:S(2)}) %collective-permute-start.16) | collective-permute-done | bytes 131104 | tf_op jit(solution)/shard_map/ppermute | solution.py:54
  107.2 2.4 %dense_middle.1 = (bf16[256,256]{1,0:T(8,128)(2,1)}, bf16[256,256]{1,0:T(8,128)(2,1)}, f32[256,256]{1,0:T(8,128)}) custom-call(bf16[256,256]{1,0:T(8,128)(2,1)} %get-tuple-element.32.own, bf16[256,256]{1,0:T(8,128)(2,1)} %copy-done.9, bf16[256,256]{1,0:T(8,128)(2,1)} %copy-done.10, bf16[256,256]{1,0:T(8,128)(2,1)} %copy-done.11, f32[256,256]{1,0:T(8,128)} %mul.77.inv, ...), custom_call_target="tpu_custom_call" | custom-call | tf_op jit(solution)/shard_map/dense_middle/pallas_call | solution.py:177
  109.6 3.8 %collective-permute-start.18 = (bf16[256,256]{1,0:T(8,128)(2,1)}, bf16[256,256]{1,0:T(8,128)(2,1)S(1)}, u32[]{:S(2)}, u32[]{:S(2)}) collective-permute-start(bf16[256,256]{1,0:T(8,128)(2,1)} %get-tuple-element.9), channel_id=1, source_target_pairs={{0,6},{1,7},{2,0},{3,1},{4,2},{5,3},{6,4},{7,5},{8,14},{9,15},{10,... | collective-permute-start | bytes 393224 | tf_op jit(solution)/shard_map/ppermute | solution.py:54
  114.5 3.5 %collective-permute-done.17 = bf16[256,256]{1,0:T(8,128)(2,1)S(1)} collective-permute-done((bf16[256,256]{1,0:T(8,128)(2,1)}, bf16[256,256]{1,0:T(8,128)(2,1)S(1)}, u32[]{:S(2)}, u32[]{:S(2)}) %collective-permute-start.17) | collective-permute-done | bytes 131104 | tf_op jit(solution)/shard_map/ppermute | solution.py:54
  118.1 6.1 %collective-permute-done.19 = bf16[256,256]{1,0:T(8,128)(2,1)S(1)} collective-permute-done((bf16[256,256]{1,0:T(8,128)(2,1)}, bf16[256,256]{1,0:T(8,128)(2,1)S(1)}, u32[]{:S(2)}, u32[]{:S(2)}) %collective-permute-start.19) | collective-permute-done | bytes 131104 | tf_op jit(solution)/shard_map/ppermute | solution.py:54
  127.1 16.2 %backward_product.1 = (bf16[32,136,256]{2,1,0:T(8,128)(2,1)}, bf16[32,128,256]{2,1,0:T(8,128)(2,1)}) custom-call(s32[48]{0:T(128)} %pad_add_fusion.chunks, s32[256]{0:T(256)} %reshape.99.cols, s32[16]{0:T(128)} %lens.3, bf16[16,16,128,128]{3,2,1,0:T(8,128)(2,1)} %tiles.3, bf16[8,128,256]{2,1,0:T(8,128)(2,1)} %bitcast.38, bf16[8,128,256]{2,1,0:T(8,128)(2,1)} %bitcast.50, ...), custom_call_target="tpu_custom_call" | custom-call | flops 2147483648 | bytes 16777216 | tf_op jit(solution)/shard_map/backward_product/pallas_call | solution.py:240
  145.1 3.2 %collective-permute-start.29 = (bf16[1024,256]{1,0:T(8,128)(2,1)S(1)}, bf16[1024,256]{1,0:T(8,128)(2,1)S(1)}, u32[]{:S(2)}, u32[]{:S(2)}) collective-permute-start(bf16[1024,256]{1,0:T(8,128)(2,1)S(1)} %bitcast.49), channel_id=1, source_target_pairs={{0,32},{8,40},{16,48},{24,56},{32,0},{40,8},{48,16},{56,24},{64,96... | collective-permute-start | bytes 1572872 | tf_op jit(solution)/shard_map/ppermute | solution.py:33
  148.2 7.3 %collective-permute-start.28 = (bf16[1024,256]{1,0:T(8,128)(2,1)S(1)}, bf16[1024,256]{1,0:T(8,128)(2,1)S(1)}, u32[]{:S(2)}, u32[]{:S(2)}) collective-permute-start(bf16[1024,256]{1,0:T(8,128)(2,1)S(1)} %bitcast.48), channel_id=1, source_target_pairs={{0,48},{8,56},{16,0},{24,8},{32,16},{40,24},{48,32},{56,40},{64,11... | collective-permute-start | bytes 1572872 | tf_op jit(solution)/shard_map/ppermute | solution.py:33
  155.9 3.0 %collective-permute-done.29 = bf16[1024,256]{1,0:T(8,128)(2,1)S(1)} collective-permute-done((bf16[1024,256]{1,0:T(8,128)(2,1)S(1)}, bf16[1024,256]{1,0:T(8,128)(2,1)S(1)}, u32[]{:S(2)}, u32[]{:S(2)}) %collective-permute-start.29) | collective-permute-done | bytes 524320 | tf_op jit(solution)/shard_map/ppermute | solution.py:33
  159.0 3.6 %collective-permute-start.21 = (bf16[1088,256]{1,0:T(8,128)(2,1)S(1)}, bf16[1088,256]{1,0:T(8,128)(2,1)S(1)}, u32[]{:S(2)}, u32[]{:S(2)}) collective-permute-start(bf16[1088,256]{1,0:T(8,128)(2,1)S(1)} %bitcast.39), channel_id=1, source_target_pairs={{0,64},{8,72},{16,80},{24,88},{32,96},{40,104},{48,112},{56,120},{... | collective-permute-start | bytes 1671176 | tf_op jit(solution)/shard_map/ppermute | solution.py:33
  162.5 12.2 %collective-permute-done.28 = bf16[1024,256]{1,0:T(8,128)(2,1)S(1)} collective-permute-done((bf16[1024,256]{1,0:T(8,128)(2,1)S(1)}, bf16[1024,256]{1,0:T(8,128)(2,1)S(1)}, u32[]{:S(2)}, u32[]{:S(2)}) %collective-permute-start.28) | collective-permute-done | bytes 524320 | tf_op jit(solution)/shard_map/ppermute | solution.py:33
  175.1 2.0 collective-permute-start.32
  177.1 3.2 %collective-permute-start.30 = (bf16[256,256]{1,0:T(8,128)(2,1)S(1)}, bf16[256,256]{1,0:T(8,128)(2,1)S(1)}, u32[]{:S(2)}, u32[]{:S(2)}) collective-permute-start(bf16[256,256]{1,0:T(8,128)(2,1)S(1)} %get-tuple-element.26), channel_id=1, source_target_pairs={{0,64},{8,72},{16,80},{24,88},{32,96},{40,104},{48,112},{56,120},{... | collective-permute-start | bytes 393224 | tf_op jit(solution)/shard_map/ppermute | solution.py:33
  180.3 2.5 %collective-permute-done.22 = bf16[1088,256]{1,0:T(8,128)(2,1)S(1)} collective-permute-done((bf16[1088,256]{1,0:T(8,128)(2,1)S(1)}, bf16[1088,256]{1,0:T(8,128)(2,1)S(1)}, u32[]{:S(2)}, u32[]{:S(2)}) %collective-permute-start.22) | collective-permute-done | bytes 557088 | tf_op jit(solution)/shard_map/ppermute | solution.py:33
  183.5 2.9 %collective-permute-start.25 = (bf16[272,256]{1,0:T(8,128)(2,1)S(1)}, bf16[272,256]{1,0:T(8,128)(2,1)S(1)}, u32[]{:S(2)}, u32[]{:S(2)}) collective-permute-start(bf16[272,256]{1,0:T(8,128)(2,1)S(1)} %get-tuple-element.25), channel_id=1, source_target_pairs={{0,48},{8,56},{16,0},{24,8},{32,16},{40,24},{48,32},{56,40},{64,11... | collective-permute-start | bytes 417800 | tf_op jit(solution)/shard_map/ppermute | solution.py:33
  187.0 4.5 %collective-permute-done.26 = bf16[272,256]{1,0:T(8,128)(2,1)S(1)} collective-permute-done((bf16[272,256]{1,0:T(8,128)(2,1)S(1)}, bf16[272,256]{1,0:T(8,128)(2,1)S(1)}, u32[]{:S(2)}, u32[]{:S(2)}) %collective-permute-start.26) | collective-permute-done | bytes 139296 | tf_op jit(solution)/shard_map/ppermute | solution.py:33
  193.7 6.4 %collective-permute-start.33 = (bf16[264,256]{1,0:T(8,128)(2,1)S(1)}, bf16[264,256]{1,0:T(8,128)(2,1)S(1)}, u32[]{:S(2)}, u32[]{:S(2)}) collective-permute-start(bf16[264,256]{1,0:T(8,128)(2,1)S(1)} %pad_maximum_fusion.1), channel_id=1, source_target_pairs={{0,8},{8,0},{16,24},{24,16},{32,40},{40,32},{48,56},{56,48},{64,72... | collective-permute-start | bytes 405512 | tf_op jit(solution)/shard_map/ppermute | solution.py:33
  200.2 5.9 %collective-permute-done.33 = bf16[264,256]{1,0:T(8,128)(2,1)S(1)} collective-permute-done((bf16[264,256]{1,0:T(8,128)(2,1)S(1)}, bf16[264,256]{1,0:T(8,128)(2,1)S(1)}, u32[]{:S(2)}, u32[]{:S(2)}) %collective-permute-start.33) | collective-permute-done | bytes 135200 | tf_op jit(solution)/shard_map/ppermute | solution.py:33
  (114 shorter events, 39.3 us)
Async XLA Ops:
  2.3 11.9 %collective-permute-start.2 = (bf16[256,256]{1,0:T(8,128)(2,1)S(1)}, bf16[256,256]{1,0:T(8,128)(2,1)S(1)}, u32[]{:S(2)}, u32[]{:S(2)}) collective-permute-start(bf16[256,256]{1,0:T(8,128)(2,1)S(1)} %multiply_convert_fusion), channel_id=1, source_target_pairs={{0,128},{8,136},{16,144},{24,152},{32,160},{40,168},{48,176},{56,1... | collective-permute-start | bytes 393224 | tf_op jit(solution)/shard_map/ppermute | solution.py:33
  3.8 10.4 %collective-permute-start.1 = (bf16[256,256]{1,0:T(8,128)(2,1)S(1)}, bf16[256,256]{1,0:T(8,128)(2,1)S(1)}, u32[]{:S(2)}, u32[]{:S(2)}) collective-permute-start(bf16[256,256]{1,0:T(8,128)(2,1)S(1)} %multiply_convert_fusion), channel_id=1, source_target_pairs={{0,192},{8,200},{16,208},{24,216},{32,224},{40,232},{48,240},{56,2... | collective-permute-start | bytes 393224 | tf_op jit(solution)/shard_map/ppermute | solution.py:33
  5.5 8.8 %collective-permute-start = (bf16[256,256]{1,0:T(8,128)(2,1)S(1)}, bf16[256,256]{1,0:T(8,128)(2,1)S(1)}, u32[]{:S(2)}, u32[]{:S(2)}) collective-permute-start(bf16[256,256]{1,0:T(8,128)(2,1)S(1)} %multiply_convert_fusion), channel_id=1, source_target_pairs={{0,64},{8,72},{16,80},{24,88},{32,96},{40,104},{48,112},{56,120},{... | collective-permute-start | bytes 393224 | tf_op jit(solution)/shard_map/ppermute | solution.py:33
  7.1 11.6 %collective-permute-start.6 = (bf16[256,256]{1,0:T(8,128)(2,1)S(1)}, bf16[256,256]{1,0:T(8,128)(2,1)S(1)}, u32[]{:S(2)}, u32[]{:S(2)}) collective-permute-start(bf16[256,256]{1,0:T(8,128)(2,1)S(1)} %multiply_convert_fusion), channel_id=1, source_target_pairs={{0,8},{8,0},{16,24},{24,16},{32,40},{40,32},{48,56},{56,48},{64,72... | collective-permute-start | bytes 393224 | tf_op jit(solution)/shard_map/ppermute | solution.py:33
  14.3 36.3 %collective-permute-start.3 = (bf16[1024,256]{1,0:T(8,128)(2,1)S(1)}, bf16[1024,256]{1,0:T(8,128)(2,1)S(1)}, u32[]{:S(2)}, u32[]{:S(2)}) collective-permute-start(bf16[1024,256]{1,0:T(8,128)(2,1)S(1)} %pad_maximum_fusion), channel_id=1, source_target_pairs={{0,16},{8,24},{16,32},{24,40},{32,48},{40,56},{48,0},{56,8},{64,80... | collective-permute-start | bytes 1572872 | tf_op jit(solution)/shard_map/ppermute | solution.py:33
  18.7 13.5 %collective-permute-start.7 = (bf16[256,256]{1,0:T(8,128)(2,1)S(1)}, bf16[256,256]{1,0:T(8,128)(2,1)S(1)}, u32[]{:S(2)}, u32[]{:S(2)}) collective-permute-start(bf16[256,256]{1,0:T(8,128)(2,1)S(1)} %collective-permute-done.6), channel_id=1, source_target_pairs={{0,16},{8,24},{16,32},{24,40},{32,48},{40,56},{48,0},{56,8},{64,80... | collective-permute-start | bytes 393224 | tf_op jit(solution)/shard_map/ppermute | solution.py:33
  20.2 32.6 %collective-permute-start.4 = (bf16[1024,256]{1,0:T(8,128)(2,1)S(1)}, bf16[1024,256]{1,0:T(8,128)(2,1)S(1)}, u32[]{:S(2)}, u32[]{:S(2)}) collective-permute-start(bf16[1024,256]{1,0:T(8,128)(2,1)S(1)} %pad_maximum_fusion), channel_id=1, source_target_pairs={{0,48},{8,56},{16,0},{24,8},{32,16},{40,24},{48,32},{56,40},{64,11... | collective-permute-start | bytes 1572872 | tf_op jit(solution)/shard_map/ppermute | solution.py:33
  21.9 30.9 %collective-permute-start.5 = (bf16[1024,256]{1,0:T(8,128)(2,1)S(1)}, bf16[1024,256]{1,0:T(8,128)(2,1)S(1)}, u32[]{:S(2)}, u32[]{:S(2)}) collective-permute-start(bf16[1024,256]{1,0:T(8,128)(2,1)S(1)} %pad_maximum_fusion), channel_id=1, source_target_pairs={{0,32},{8,40},{16,48},{24,56},{32,0},{40,8},{48,16},{56,24},{64,96... | collective-permute-start | bytes 1572872 | tf_op jit(solution)/shard_map/ppermute | solution.py:33
  23.9 22.2 %collective-permute-start.8 = (bf16[256,256]{1,0:T(8,128)(2,1)S(1)}, bf16[256,256]{1,0:T(8,128)(2,1)S(1)}, u32[]{:S(2)}, u32[]{:S(2)}) collective-permute-start(bf16[256,256]{1,0:T(8,128)(2,1)S(1)} %collective-permute-done.6), channel_id=1, source_target_pairs={{0,48},{8,56},{16,0},{24,8},{32,16},{40,24},{48,32},{56,40},{64,11... | collective-permute-start | bytes 393224 | tf_op jit(solution)/shard_map/ppermute | solution.py:33
  32.2 16.4 %collective-permute-start.9 = (bf16[256,256]{1,0:T(8,128)(2,1)S(1)}, bf16[256,256]{1,0:T(8,128)(2,1)S(1)}, u32[]{:S(2)}, u32[]{:S(2)}) collective-permute-start(bf16[256,256]{1,0:T(8,128)(2,1)S(1)} %collective-permute-done.6), channel_id=1, source_target_pairs={{0,32},{8,40},{16,48},{24,56},{32,0},{40,8},{48,16},{56,24},{64,96... | collective-permute-start | bytes 393224 | tf_op jit(solution)/shard_map/ppermute | solution.py:33
  48.6 14.9 %collective-permute-start.10 = (bf16[1024,256]{1,0:T(8,128)(2,1)S(1)}, bf16[1024,256]{1,0:T(8,128)(2,1)S(1)}, u32[]{:S(2)}, u32[]{:S(2)}) collective-permute-start(bf16[1024,256]{1,0:T(8,128)(2,1)S(1)} %constant_dynamic-update-slice_fusion), channel_id=1, source_target_pairs={{0,64},{8,72},{16,80},{24,88},{32,96},{40,104},{48,112},{56,120},{... | collective-permute-start | bytes 1572872 | tf_op jit(solution)/shard_map/ppermute | solution.py:33
  49.5 21.6 %collective-permute-start.11 = (bf16[1024,256]{1,0:T(8,128)(2,1)S(1)}, bf16[1024,256]{1,0:T(8,128)(2,1)}, u32[]{:S(2)}, u32[]{:S(2)}) collective-permute-start(bf16[1024,256]{1,0:T(8,128)(2,1)S(1)} %constant_dynamic-update-slice_fusion), channel_id=1, source_target_pairs={{0,192},{8,200},{16,208},{24,216},{32,224},{40,232},{48,240},{56,2... | collective-permute-start | bytes 1572872 | tf_op jit(solution)/shard_map/ppermute | solution.py:33
  50.7 20.5 %collective-permute-start.12 = (bf16[1024,256]{1,0:T(8,128)(2,1)S(1)}, bf16[1024,256]{1,0:T(8,128)(2,1)}, u32[]{:S(2)}, u32[]{:S(2)}) collective-permute-start(bf16[1024,256]{1,0:T(8,128)(2,1)S(1)} %constant_dynamic-update-slice_fusion), channel_id=1, source_target_pairs={{0,128},{8,136},{16,144},{24,152},{32,160},{40,168},{48,176},{56,1... | collective-permute-start | bytes 1572872 | tf_op jit(solution)/shard_map/ppermute | solution.py:33
  90.3 8.1 %collective-permute-start.14 = (bf16[256,256]{1,0:T(8,128)(2,1)S(1)}, bf16[256,256]{1,0:T(8,128)(2,1)S(1)}, u32[]{:S(2)}, u32[]{:S(2)}) collective-permute-start(bf16[256,256]{1,0:T(8,128)(2,1)S(1)} %get-tuple-element.31), channel_id=1, source_target_pairs={{0,2},{1,3},{2,4},{3,5},{4,6},{5,7},{6,0},{7,1},{8,10},{9,11},{10,... | collective-permute-start | bytes 393224 | tf_op jit(solution)/shard_map/ppermute | solution.py:54
  91.6 9.1 %collective-permute-start.15 = (bf16[256,256]{1,0:T(8,128)(2,1)S(1)}, bf16[256,256]{1,0:T(8,128)(2,1)S(1)}, u32[]{:S(2)}, u32[]{:S(2)}) collective-permute-start(bf16[256,256]{1,0:T(8,128)(2,1)S(1)} %get-tuple-element.30), channel_id=1, source_target_pairs={{0,6},{1,7},{2,0},{3,1},{4,2},{5,3},{6,4},{7,5},{8,14},{9,15},{10,... | collective-permute-start | bytes 393224 | tf_op jit(solution)/shard_map/ppermute | solution.py:54
  94.2 12.2 %collective-permute-start.16 = (bf16[256,256]{1,0:T(8,128)(2,1)S(1)}, bf16[256,256]{1,0:T(8,128)(2,1)S(1)}, u32[]{:S(2)}, u32[]{:S(2)}) collective-permute-start(bf16[256,256]{1,0:T(8,128)(2,1)S(1)} %get-tuple-element.29), channel_id=1, source_target_pairs={{0,4},{1,5},{2,6},{3,7},{4,0},{5,1},{6,2},{7,3},{8,12},{9,13},{10,... | collective-permute-start | bytes 393224 | tf_op jit(solution)/shard_map/ppermute | solution.py:54
  109.6 8.4 %collective-permute-start.17 = (bf16[256,256]{1,0:T(8,128)(2,1)}, bf16[256,256]{1,0:T(8,128)(2,1)S(1)}, u32[]{:S(2)}, u32[]{:S(2)}) collective-permute-start(bf16[256,256]{1,0:T(8,128)(2,1)} %get-tuple-element.9), channel_id=1, source_target_pairs={{0,2},{1,3},{2,4},{3,5},{4,6},{5,7},{6,0},{7,1},{8,10},{9,11},{10,... | collective-permute-start | bytes 393224 | tf_op jit(solution)/shard_map/ppermute | solution.py:54
  109.6 8.5 %collective-permute-start.18 = (bf16[256,256]{1,0:T(8,128)(2,1)}, bf16[256,256]{1,0:T(8,128)(2,1)S(1)}, u32[]{:S(2)}, u32[]{:S(2)}) collective-permute-start(bf16[256,256]{1,0:T(8,128)(2,1)} %get-tuple-element.9), channel_id=1, source_target_pairs={{0,6},{1,7},{2,0},{3,1},{4,2},{5,3},{6,4},{7,5},{8,14},{9,15},{10,... | collective-permute-start | bytes 393224 | tf_op jit(solution)/shard_map/ppermute | solution.py:54
  114.4 9.8 %collective-permute-start.19 = (bf16[256,256]{1,0:T(8,128)(2,1)}, bf16[256,256]{1,0:T(8,128)(2,1)S(1)}, u32[]{:S(2)}, u32[]{:S(2)}) collective-permute-start(bf16[256,256]{1,0:T(8,128)(2,1)} %get-tuple-element.9), channel_id=1, source_target_pairs={{0,4},{1,5},{2,6},{3,7},{4,0},{5,1},{6,2},{7,3},{8,12},{9,13},{10,... | collective-permute-start | bytes 393224 | tf_op jit(solution)/shard_map/ppermute | solution.py:54
  145.1 13.9 %collective-permute-start.29 = (bf16[1024,256]{1,0:T(8,128)(2,1)S(1)}, bf16[1024,256]{1,0:T(8,128)(2,1)S(1)}, u32[]{:S(2)}, u32[]{:S(2)}) collective-permute-start(bf16[1024,256]{1,0:T(8,128)(2,1)S(1)} %bitcast.49), channel_id=1, source_target_pairs={{0,32},{8,40},{16,48},{24,56},{32,0},{40,8},{48,16},{56,24},{64,96... | collective-permute-start | bytes 1572872 | tf_op jit(solution)/shard_map/ppermute | solution.py:33
  148.2 26.5 %collective-permute-start.28 = (bf16[1024,256]{1,0:T(8,128)(2,1)S(1)}, bf16[1024,256]{1,0:T(8,128)(2,1)S(1)}, u32[]{:S(2)}, u32[]{:S(2)}) collective-permute-start(bf16[1024,256]{1,0:T(8,128)(2,1)S(1)} %bitcast.48), channel_id=1, source_target_pairs={{0,48},{8,56},{16,0},{24,8},{32,16},{40,24},{48,32},{56,40},{64,11... | collective-permute-start | bytes 1572872 | tf_op jit(solution)/shard_map/ppermute | solution.py:33
  155.6 19.2 %collective-permute-start.27 = (bf16[1024,256]{1,0:T(8,128)(2,1)S(1)}, bf16[1024,256]{1,0:T(8,128)(2,1)S(1)}, u32[]{:S(2)}, u32[]{:S(2)}) collective-permute-start(bf16[1024,256]{1,0:T(8,128)(2,1)S(1)} %bitcast.47), channel_id=1, source_target_pairs={{0,16},{8,24},{16,32},{24,40},{32,48},{40,56},{48,0},{56,8},{64,80... | collective-permute-start | bytes 1572872 | tf_op jit(solution)/shard_map/ppermute | solution.py:33
  155.7 21.3 %collective-permute-start.23 = (bf16[1088,256]{1,0:T(8,128)(2,1)S(1)}, bf16[1088,256]{1,0:T(8,128)(2,1)S(1)}, u32[]{:S(2)}, u32[]{:S(2)}) collective-permute-start(bf16[1088,256]{1,0:T(8,128)(2,1)S(1)} %bitcast.41), channel_id=1, source_target_pairs={{0,128},{8,136},{16,144},{24,152},{32,160},{40,168},{48,176},{56,1... | collective-permute-start | bytes 1671176 | tf_op jit(solution)/shard_map/ppermute | solution.py:33
  155.8 27.0 %collective-permute-start.22 = (bf16[1088,256]{1,0:T(8,128)(2,1)S(1)}, bf16[1088,256]{1,0:T(8,128)(2,1)S(1)}, u32[]{:S(2)}, u32[]{:S(2)}) collective-permute-start(bf16[1088,256]{1,0:T(8,128)(2,1)S(1)} %bitcast.40), channel_id=1, source_target_pairs={{0,192},{8,200},{16,208},{24,216},{32,224},{40,232},{48,240},{56,2... | collective-permute-start | bytes 1671176 | tf_op jit(solution)/shard_map/ppermute | solution.py:33
  159.0 23.9 %collective-permute-start.21 = (bf16[1088,256]{1,0:T(8,128)(2,1)S(1)}, bf16[1088,256]{1,0:T(8,128)(2,1)S(1)}, u32[]{:S(2)}, u32[]{:S(2)}) collective-permute-start(bf16[1088,256]{1,0:T(8,128)(2,1)S(1)} %bitcast.39), channel_id=1, source_target_pairs={{0,64},{8,72},{16,80},{24,88},{32,96},{40,104},{48,112},{56,120},{... | collective-permute-start | bytes 1671176 | tf_op jit(solution)/shard_map/ppermute | solution.py:33
  175.1 11.4 %collective-permute-start.32 = (bf16[256,256]{1,0:T(8,128)(2,1)S(1)}, bf16[256,256]{1,0:T(8,128)(2,1)S(1)}, u32[]{:S(2)}, u32[]{:S(2)}) collective-permute-start(bf16[256,256]{1,0:T(8,128)(2,1)S(1)} %get-tuple-element.27), channel_id=1, source_target_pairs={{0,128},{8,136},{16,144},{24,152},{32,160},{40,168},{48,176},{56,1... | collective-permute-start | bytes 393224 | tf_op jit(solution)/shard_map/ppermute | solution.py:33
  177.1 9.9 %collective-permute-start.31 = (bf16[256,256]{1,0:T(8,128)(2,1)S(1)}, bf16[256,256]{1,0:T(8,128)(2,1)S(1)}, u32[]{:S(2)}, u32[]{:S(2)}) collective-permute-start(bf16[256,256]{1,0:T(8,128)(2,1)S(1)} %get-tuple-element.28), channel_id=1, source_target_pairs={{0,192},{8,200},{16,208},{24,216},{32,224},{40,232},{48,240},{56,2... | collective-permute-start | bytes 393224 | tf_op jit(solution)/shard_map/ppermute | solution.py:33
  177.1 9.9 %collective-permute-start.30 = (bf16[256,256]{1,0:T(8,128)(2,1)S(1)}, bf16[256,256]{1,0:T(8,128)(2,1)S(1)}, u32[]{:S(2)}, u32[]{:S(2)}) collective-permute-start(bf16[256,256]{1,0:T(8,128)(2,1)S(1)} %get-tuple-element.26), channel_id=1, source_target_pairs={{0,64},{8,72},{16,80},{24,88},{32,96},{40,104},{48,112},{56,120},{... | collective-permute-start | bytes 393224 | tf_op jit(solution)/shard_map/ppermute | solution.py:33
  183.2 8.4 %collective-permute-start.26 = (bf16[272,256]{1,0:T(8,128)(2,1)S(1)}, bf16[272,256]{1,0:T(8,128)(2,1)S(1)}, u32[]{:S(2)}, u32[]{:S(2)}) collective-permute-start(bf16[272,256]{1,0:T(8,128)(2,1)S(1)} %get-tuple-element.24), channel_id=1, source_target_pairs={{0,32},{8,40},{16,48},{24,56},{32,0},{40,8},{48,16},{56,24},{64,96... | collective-permute-start | bytes 417800 | tf_op jit(solution)/shard_map/ppermute | solution.py:33
  183.5 9.0 %collective-permute-start.25 = (bf16[272,256]{1,0:T(8,128)(2,1)S(1)}, bf16[272,256]{1,0:T(8,128)(2,1)S(1)}, u32[]{:S(2)}, u32[]{:S(2)}) collective-permute-start(bf16[272,256]{1,0:T(8,128)(2,1)S(1)} %get-tuple-element.25), channel_id=1, source_target_pairs={{0,48},{8,56},{16,0},{24,8},{32,16},{40,24},{48,32},{56,40},{64,11... | collective-permute-start | bytes 417800 | tf_op jit(solution)/shard_map/ppermute | solution.py:33
  186.5 7.1 %collective-permute-start.24 = (bf16[272,256]{1,0:T(8,128)(2,1)S(1)}, bf16[272,256]{1,0:T(8,128)(2,1)S(1)}, u32[]{:S(2)}, u32[]{:S(2)}) collective-permute-start(bf16[272,256]{1,0:T(8,128)(2,1)S(1)} %get-tuple-element.23), channel_id=1, source_target_pairs={{0,16},{8,24},{16,32},{24,40},{32,48},{40,56},{48,0},{56,8},{64,80... | collective-permute-start | bytes 417800 | tf_op jit(solution)/shard_map/ppermute | solution.py:33
  193.7 12.4 %collective-permute-start.33 = (bf16[264,256]{1,0:T(8,128)(2,1)S(1)}, bf16[264,256]{1,0:T(8,128)(2,1)S(1)}, u32[]{:S(2)}, u32[]{:S(2)}) collective-permute-start(bf16[264,256]{1,0:T(8,128)(2,1)S(1)} %pad_maximum_fusion.1), channel_id=1, source_target_pairs={{0,8},{8,0},{16,24},{24,16},{32,40},{40,32},{48,56},{56,48},{64,72... | collective-permute-start | bytes 405512 | tf_op jit(solution)/shard_map/ppermute | solution.py:33
  (19 other events, 244.4 us)

commit v2 on v1

--- a/solution.py
+++ b/solution.py
@@ -71,7 +71,9 @@
     first, second = own, flip_z(own)
     firsts = [first] + [shift_x(first, step) for step in SHIFTS]
     seconds = [second] + [shift_y(second, step) for step in SHIFTS]
-    first, second = jnp.concatenate(firsts), jnp.concatenate(seconds)
+    first, second = lax.optimization_barrier(
+        (jnp.concatenate(firsts), jnp.concatenate(seconds))
+    )
     firsts = [first] + [shift_y(first, step) for step in SHIFTS]
     seconds = [second] + [shift_x(second, step) for step in SHIFTS]
     return firsts + seconds

time: 217 us -> 199 us (0.917)
  starting transfers between devices: 77.6 us -> 56.5 us
  waiting for transfers between devices: 88.6 us -> 91.2 us
  Pallas kernels: 33.6 us -> 35.9 us
    ppermute x26, starting transfers between devices: 65.4 us -> 45.5 us  [row_shift(): return lax.ppermute(value, 'row', pairs)]
    pallas_call x1, Pallas kernels: 16.2 us -> 18.4 us  [backward(): pl.pallas_call(backward_kernel, name='backward_product', out_shape=(jax.S...]
  transfers between devices with their start and end apart: 38 -> 38, of which waited for: 25 -> 23; matrix products, arithmetic and copies ran while one was open for 2% -> 3% of each run, Pallas kernels for 0% -> 0%
where the time goes in v2:
time: 199 us; the launch traced here: 198 us
  waiting for transfers between devices  91.2 us (46%)
  starting transfers between devices  56.5 us (28%)
  Pallas kernels  35.9 us (18%)
  local copies, waits for them, and re-layouts  7.95 us (4%)
  other arithmetic  5.29 us (3%)
    ppermute x26, waiting for transfers between devices, row_shift(): return lax.ppermute(value, 'row', pairs)  63.3 us
    ppermute x26, starting transfers between devices, row_shift(): return lax.ppermute(value, 'row', pairs)  45.5 us
    ppermute x9, waiting for transfers between devices, shift_run(): return lax.ppermute(value, 'rep', pairs)  24.2 us
    pallas_call x1, Pallas kernels, backward(): pl.pallas_call(backward_kernel, name='backward_product', out_shape=(jax.S...  18.4 us
    pallas_call x1, Pallas kernels, forward(): pl.pallas_call(forward_kernel, name='forward_product', out_shape=jax.Shap...  15.1 us
    ppermute x9, starting transfers between devices, shift_run(): return lax.ppermute(value, 'rep', pairs)  10.7 us
  transfers between devices with their start and end apart: 38, of which 23 were waited for; matrix products, arithmetic and copies ran while one was open for 3% of the time, Pallas kernels for 0%

profile of v2, /device:TPU:6, one launch (start us, length us, event | category | flops | bytes accessed | tf_op | source)
XLA Modules:
  0.0 197.8 jit_solution(6317262682448880711)
XLA Ops:
  2.3 7.3 %collective-permute-start.3 = (bf16[256,256]{1,0:T(8,128)(2,1)S(1)}, bf16[256,256]{1,0:T(8,128)(2,1)S(1)}, u32[]{:S(2)}, u32[]{:S(2)}) collective-permute-start(bf16[256,256]{1,0:T(8,128)(2,1)S(1)} %multiply_convert_fusion), channel_id=1, source_target_pairs={{0,8},{8,0},{16,24},{24,16},{32,40},{40,32},{48,56},{56,48},{64,72... | collective-permute-start | bytes 393224 | tf_op jit(solution)/shard_map/ppermute | solution.py:33
  11.0 3.2 %collective-permute-start = (bf16[256,256]{1,0:T(8,128)(2,1)S(1)}, bf16[256,256]{1,0:T(8,128)(2,1)S(1)}, u32[]{:S(2)}, u32[]{:S(2)}) collective-permute-start(bf16[256,256]{1,0:T(8,128)(2,1)S(1)} %multiply_convert_fusion), channel_id=1, source_target_pairs={{0,64},{8,72},{16,80},{24,88},{32,96},{40,104},{48,112},{56,120},{... | collective-permute-start | bytes 393224 | tf_op jit(solution)/shard_map/ppermute | solution.py:33
  14.3 3.2 %collective-permute-start.6 = (bf16[256,256]{1,0:T(8,128)(2,1)S(1)}, bf16[256,256]{1,0:T(8,128)(2,1)S(1)}, u32[]{:S(2)}, u32[]{:S(2)}) collective-permute-start(bf16[256,256]{1,0:T(8,128)(2,1)S(1)} %collective-permute-done.3), channel_id=1, source_target_pairs={{0,32},{8,40},{16,48},{24,56},{32,0},{40,8},{48,16},{56,24},{64,96... | collective-permute-start | bytes 393224 | tf_op jit(solution)/shard_map/ppermute | solution.py:33
  19.5 2.3 %collective-permute-done.6 = bf16[256,256]{1,0:T(8,128)(2,1)S(1)} collective-permute-done((bf16[256,256]{1,0:T(8,128)(2,1)S(1)}, bf16[256,256]{1,0:T(8,128)(2,1)S(1)}, u32[]{:S(2)}, u32[]{:S(2)}) %collective-permute-start.6) | collective-permute-done | bytes 131104 | tf_op jit(solution)/shard_map/ppermute | solution.py:33
  24.8 3.2 %collective-permute-start.8 = (bf16[1024,256]{1,0:T(8,128)(2,1)S(1)}, bf16[1024,256]{1,0:T(8,128)(2,1)S(1)}, u32[]{:S(2)}, u32[]{:S(2)}) collective-permute-start(bf16[1024,256]{1,0:T(8,128)(2,1)S(1)} %pad_maximum_fusion), channel_id=1, source_target_pairs={{0,48},{8,56},{16,0},{24,8},{32,16},{40,24},{48,32},{56,40},{64,11... | collective-permute-start | bytes 1572872 | tf_op jit(solution)/shard_map/ppermute | solution.py:33
  30.1 18.7 %collective-permute-done.7 = bf16[1024,256]{1,0:T(8,128)(2,1)S(1)} collective-permute-done((bf16[1024,256]{1,0:T(8,128)(2,1)S(1)}, bf16[1024,256]{1,0:T(8,128)(2,1)S(1)}, u32[]{:S(2)}, u32[]{:S(2)}) %collective-permute-start.7) | collective-permute-done | bytes 524320 | tf_op jit(solution)/shard_map/ppermute | solution.py:33
  50.7 8.9 %collective-permute-done.12 = bf16[1024,256]{1,0:T(8,128)(2,1)} collective-permute-done((bf16[1024,256]{1,0:T(8,128)(2,1)S(1)}, bf16[1024,256]{1,0:T(8,128)(2,1)}, u32[]{:S(2)}, u32[]{:S(2)}) %collective-permute-start.12) | collective-permute-done | bytes 524320 | tf_op jit(solution)/shard_map/ppermute | solution.py:33
  59.6 15.1 %forward_product.1 = bf16[16,128,256]{2,1,0:T(8,128)(2,1)} custom-call(s32[16]{0:T(128)} %multiply_add_fusion.2.lists, s32[256]{0:T(256)} %reshape.90.cols, s32[16]{0:T(128)} %lens.3, bf16[16,16,128,128]{3,2,1,0:T(8,128)(2,1)} %tiles.3, bf16[8,128,256]{2,1,0:T(8,128)(2,1)} %bitcast.35, bf16[8,128,256]{2,1,0:T(8,128)(2,1)} %bitcast.42, ...), custom_call_target="tpu_custom_call" | custom-call | flops 2147483648 | bytes 12582912 | tf_op jit(solution)/shard_map/forward_product/pallas_call | solution.py:131
  76.1 1.9 collective-permute-done.13
  78.8 1.9 collective-permute-start.14
  80.7 2.0 collective-permute-start.15
  82.7 4.4 %collective-permute-done.14.one = bf16[256,256]{1,0:T(8,128)(2,1)S(1)} collective-permute-done((bf16[256,256]{1,0:T(8,128)(2,1)S(1)}, bf16[256,256]{1,0:T(8,128)(2,1)S(1)}, u32[]{:S(2)}, u32[]{:S(2)}) %collective-permute-start.14) | collective-permute-done | bytes 131104 | tf_op jit(solution)/shard_map/ppermute | solution.py:54
  87.0 2.1 %collective-permute-done.15.two = bf16[256,256]{1,0:T(8,128)(2,1)S(1)} collective-permute-done((bf16[256,256]{1,0:T(8,128)(2,1)S(1)}, bf16[256,256]{1,0:T(8,128)(2,1)S(1)}, u32[]{:S(2)}, u32[]{:S(2)}) %collective-permute-start.15) | collective-permute-done | bytes 131104 | tf_op jit(solution)/shard_map/ppermute | solution.py:54
  89.2 4.9 %collective-permute-done.16.three = bf16[256,256]{1,0:T(8,128)(2,1)S(1)} collective-permute-done((bf16[256,256]{1,0:T(8,128)(2,1)S(1)}, bf16[256,256]{1,0:T(8,128)(2,1)S(1)}, u32[]{:S(2)}, u32[]{:S(2)}) %collective-permute-start.16) | collective-permute-done | bytes 131104 | tf_op jit(solution)/shard_map/ppermute | solution.py:54
  94.9 2.4 %dense_middle.1 = (bf16[256,256]{1,0:T(8,128)(2,1)}, bf16[256,256]{1,0:T(8,128)(2,1)}, f32[256,256]{1,0:T(8,128)}) custom-call(bf16[256,256]{1,0:T(8,128)(2,1)} %get-tuple-element.36.own, bf16[256,256]{1,0:T(8,128)(2,1)} %copy-done.9, bf16[256,256]{1,0:T(8,128)(2,1)} %copy-done.10, bf16[256,256]{1,0:T(8,128)(2,1)} %copy-done.11, f32[256,256]{1,0:T(8,128)} %mul.77.inv, ...), custom_call_target="tpu_custom_call" | custom-call | tf_op jit(solution)/shard_map/dense_middle/pallas_call | solution.py:179
  97.3 3.8 %collective-permute-start.18 = (bf16[256,256]{1,0:T(8,128)(2,1)}, bf16[256,256]{1,0:T(8,128)(2,1)S(1)}, u32[]{:S(2)}, u32[]{:S(2)}) collective-permute-start(bf16[256,256]{1,0:T(8,128)(2,1)} %get-tuple-element.13), channel_id=1, source_target_pairs={{0,6},{1,7},{2,0},{3,1},{4,2},{5,3},{6,4},{7,5},{8,14},{9,15},{10,... | collective-permute-start | bytes 393224 | tf_op jit(solution)/shard_map/ppermute | solution.py:54
  102.2 3.6 %collective-permute-done.17 = bf16[256,256]{1,0:T(8,128)(2,1)S(1)} collective-permute-done((bf16[256,256]{1,0:T(8,128)(2,1)}, bf16[256,256]{1,0:T(8,128)(2,1)S(1)}, u32[]{:S(2)}, u32[]{:S(2)}) %collective-permute-start.17) | collective-permute-done | bytes 131104 | tf_op jit(solution)/shard_map/ppermute | solution.py:54
  105.8 5.1 %collective-permute-done.19 = bf16[256,256]{1,0:T(8,128)(2,1)S(1)} collective-permute-done((bf16[256,256]{1,0:T(8,128)(2,1)}, bf16[256,256]{1,0:T(8,128)(2,1)S(1)}, u32[]{:S(2)}, u32[]{:S(2)}) %collective-permute-start.19) | collective-permute-done | bytes 131104 | tf_op jit(solution)/shard_map/ppermute | solution.py:54
  113.7 18.4 %backward_product.1 = (bf16[32,136,256]{2,1,0:T(8,128)(2,1)}, bf16[32,128,256]{2,1,0:T(8,128)(2,1)}) custom-call(s32[48]{0:T(128)} %pad_add_fusion.chunks, s32[256]{0:T(256)} %reshape.99.cols, s32[16]{0:T(128)} %lens.3, bf16[16,16,128,128]{3,2,1,0:T(8,128)(2,1)} %tiles.3, bf16[8,128,256]{2,1,0:T(8,128)(2,1)} %bitcast.38, bf16[8,128,256]{2,1,0:T(8,128)(2,1)} %bitcast.50, ...), custom_call_target="tpu_custom_call" | custom-call | flops 2147483648 | bytes 16777216 | tf_op jit(solution)/shard_map/backward_product/pallas_call | solution.py:242
  132.2 1.8 fusion.37
  136.4 3.1 %collective-permute-start.22 = (bf16[1088,256]{1,0:T(8,128)(2,1)S(1)}, bf16[1088,256]{1,0:T(8,128)(2,1)S(1)}, u32[]{:S(2)}, u32[]{:S(2)}) collective-permute-start(bf16[1088,256]{1,0:T(8,128)(2,1)S(1)} %bitcast.40), channel_id=1, source_target_pairs={{0,192},{8,200},{16,208},{24,216},{32,224},{40,232},{48,240},{56,2... | collective-permute-start | bytes 1671176 | tf_op jit(solution)/shard_map/ppermute | solution.py:33
  139.5 10.8 %collective-permute-done.29 = bf16[1024,256]{1,0:T(8,128)(2,1)S(1)} collective-permute-done((bf16[1024,256]{1,0:T(8,128)(2,1)S(1)}, bf16[1024,256]{1,0:T(8,128)(2,1)S(1)}, u32[]{:S(2)}, u32[]{:S(2)}) %collective-permute-start.29) | collective-permute-done | bytes 524320 | tf_op jit(solution)/shard_map/ppermute | solution.py:33
  150.3 2.4 %collective-permute-start.21 = (bf16[1088,256]{1,0:T(8,128)(2,1)S(1)}, bf16[1088,256]{1,0:T(8,128)(2,1)S(1)}, u32[]{:S(2)}, u32[]{:S(2)}) collective-permute-start(bf16[1088,256]{1,0:T(8,128)(2,1)S(1)} %bitcast.39), channel_id=1, source_target_pairs={{0,64},{8,72},{16,80},{24,88},{32,96},{40,104},{48,112},{56,120},{... | collective-permute-start | bytes 1671176 | tf_op jit(solution)/shard_map/ppermute | solution.py:33
  152.7 4.5 %collective-permute-done.28 = bf16[1024,256]{1,0:T(8,128)(2,1)S(1)} collective-permute-done((bf16[1024,256]{1,0:T(8,128)(2,1)S(1)}, bf16[1024,256]{1,0:T(8,128)(2,1)S(1)}, u32[]{:S(2)}, u32[]{:S(2)}) %collective-permute-start.28) | collective-permute-done | bytes 524320 | tf_op jit(solution)/shard_map/ppermute | solution.py:33
  157.1 4.0 %collective-permute-done.27 = bf16[1024,256]{1,0:T(8,128)(2,1)S(1)} collective-permute-done((bf16[1024,256]{1,0:T(8,128)(2,1)S(1)}, bf16[1024,256]{1,0:T(8,128)(2,1)S(1)}, u32[]{:S(2)}, u32[]{:S(2)}) %collective-permute-start.27) | collective-permute-done | bytes 524320 | tf_op jit(solution)/shard_map/ppermute | solution.py:33
  161.6 2.6 %collective-permute-start.31 = (bf16[256,256]{1,0:T(8,128)(2,1)S(1)}, bf16[256,256]{1,0:T(8,128)(2,1)S(1)}, u32[]{:S(2)}, u32[]{:S(2)}) collective-permute-start(bf16[256,256]{1,0:T(8,128)(2,1)S(1)} %get-tuple-element.32), channel_id=1, source_target_pairs={{0,192},{8,200},{16,208},{24,216},{32,224},{40,232},{48,240},{56,2... | collective-permute-start | bytes 393224 | tf_op jit(solution)/shard_map/ppermute | solution.py:33
  165.3 4.1 %collective-permute-start.26 = (bf16[272,256]{1,0:T(8,128)(2,1)S(1)}, bf16[272,256]{1,0:T(8,128)(2,1)S(1)}, u32[]{:S(2)}, u32[]{:S(2)}) collective-permute-start(bf16[272,256]{1,0:T(8,128)(2,1)S(1)} %get-tuple-element.28), channel_id=1, source_target_pairs={{0,32},{8,40},{16,48},{24,56},{32,0},{40,8},{48,16},{56,24},{64,96... | collective-permute-start | bytes 417800 | tf_op jit(solution)/shard_map/ppermute | solution.py:33
  171.5 2.3 %collective-permute-done.26 = bf16[272,256]{1,0:T(8,128)(2,1)S(1)} collective-permute-done((bf16[272,256]{1,0:T(8,128)(2,1)S(1)}, bf16[272,256]{1,0:T(8,128)(2,1)S(1)}, u32[]{:S(2)}, u32[]{:S(2)}) %collective-permute-start.26) | collective-permute-done | bytes 139296 | tf_op jit(solution)/shard_map/ppermute | solution.py:33
  176.7 5.0 %collective-permute-start.33 = (bf16[264,256]{1,0:T(8,128)(2,1)S(1)}, bf16[264,256]{1,0:T(8,128)(2,1)S(1)}, u32[]{:S(2)}, u32[]{:S(2)}) collective-permute-start(bf16[264,256]{1,0:T(8,128)(2,1)S(1)} %pad_maximum_fusion.2), channel_id=1, source_target_pairs={{0,8},{8,0},{16,24},{24,16},{32,40},{40,32},{48,56},{56,48},{64,72... | collective-permute-start | bytes 405512 | tf_op jit(solution)/shard_map/ppermute | solution.py:33
  181.7 6.3 %collective-permute-done.33 = bf16[264,256]{1,0:T(8,128)(2,1)S(1)} collective-permute-done((bf16[264,256]{1,0:T(8,128)(2,1)S(1)}, bf16[264,256]{1,0:T(8,128)(2,1)S(1)}, u32[]{:S(2)}, u32[]{:S(2)}) %collective-permute-start.33) | collective-permute-done | bytes 135200 | tf_op jit(solution)/shard_map/ppermute | solution.py:33
  189.3 2.4 %collective-permute-start.36 = (f32[8,256]{1,0:T(8,128)S(1)}, f32[8,256]{1,0:T(8,128)S(1)}, u32[]{:S(2)}, u32[]{:S(2)}) collective-permute-start(f32[8,256]{1,0:T(8,128)S(1)} %slice_add_fusion), channel_id=1, source_target_pairs={{0,6},{1,7},{2,0},{3,1},{4,2},{5,3},{6,4},{7,5},{8,14},{9,15},{10,... | collective-permute-start | bytes 24584 | tf_op jit(solution)/shard_map/ppermute | solution.py:54
  193.9 3.2 %collective-permute-done.35 = f32[8,256]{1,0:T(8,128)S(1)} collective-permute-done((f32[8,256]{1,0:T(8,128)S(1)}, f32[8,256]{1,0:T(8,128)S(1)}, u32[]{:S(2)}, u32[]{:S(2)}) %collective-permute-start.35) | collective-permute-done | bytes 8224 | tf_op jit(solution)/shard_map/ppermute | solution.py:54
  (111 shorter events, 32.0 us)
Async XLA Ops:
  2.3 11.9 %collective-permute-start.3 = (bf16[256,256]{1,0:T(8,128)(2,1)S(1)}, bf16[256,256]{1,0:T(8,128)(2,1)S(1)}, u32[]{:S(2)}, u32[]{:S(2)}) collective-permute-start(bf16[256,256]{1,0:T(8,128)(2,1)S(1)} %multiply_convert_fusion), channel_id=1, source_target_pairs={{0,8},{8,0},{16,24},{24,16},{32,40},{40,32},{48,56},{56,48},{64,72... | collective-permute-start | bytes 393224 | tf_op jit(solution)/shard_map/ppermute | solution.py:33
  9.6 8.9 %collective-permute-start.2 = (bf16[256,256]{1,0:T(8,128)(2,1)S(1)}, bf16[256,256]{1,0:T(8,128)(2,1)S(1)}, u32[]{:S(2)}, u32[]{:S(2)}) collective-permute-start(bf16[256,256]{1,0:T(8,128)(2,1)S(1)} %multiply_convert_fusion), channel_id=1, source_target_pairs={{0,128},{8,136},{16,144},{24,152},{32,160},{40,168},{48,176},{56,1... | collective-permute-start | bytes 393224 | tf_op jit(solution)/shard_map/ppermute | solution.py:33
  11.0 8.5 %collective-permute-start.1 = (bf16[256,256]{1,0:T(8,128)(2,1)S(1)}, bf16[256,256]{1,0:T(8,128)(2,1)S(1)}, u32[]{:S(2)}, u32[]{:S(2)}) collective-permute-start(bf16[256,256]{1,0:T(8,128)(2,1)S(1)} %multiply_convert_fusion), channel_id=1, source_target_pairs={{0,192},{8,200},{16,208},{24,216},{32,224},{40,232},{48,240},{56,2... | collective-permute-start | bytes 393224 | tf_op jit(solution)/shard_map/ppermute | solution.py:33
  11.0 8.5 %collective-permute-start = (bf16[256,256]{1,0:T(8,128)(2,1)S(1)}, bf16[256,256]{1,0:T(8,128)(2,1)S(1)}, u32[]{:S(2)}, u32[]{:S(2)}) collective-permute-start(bf16[256,256]{1,0:T(8,128)(2,1)S(1)} %multiply_convert_fusion), channel_id=1, source_target_pairs={{0,64},{8,72},{16,80},{24,88},{32,96},{40,104},{48,112},{56,120},{... | collective-permute-start | bytes 393224 | tf_op jit(solution)/shard_map/ppermute | solution.py:33
  14.3 7.6 %collective-permute-start.6 = (bf16[256,256]{1,0:T(8,128)(2,1)S(1)}, bf16[256,256]{1,0:T(8,128)(2,1)S(1)}, u32[]{:S(2)}, u32[]{:S(2)}) collective-permute-start(bf16[256,256]{1,0:T(8,128)(2,1)S(1)} %collective-permute-done.3), channel_id=1, source_target_pairs={{0,32},{8,40},{16,48},{24,56},{32,0},{40,8},{48,16},{56,24},{64,96... | collective-permute-start | bytes 393224 | tf_op jit(solution)/shard_map/ppermute | solution.py:33
  17.5 5.6 %collective-permute-start.5 = (bf16[256,256]{1,0:T(8,128)(2,1)S(1)}, bf16[256,256]{1,0:T(8,128)(2,1)S(1)}, u32[]{:S(2)}, u32[]{:S(2)}) collective-permute-start(bf16[256,256]{1,0:T(8,128)(2,1)S(1)} %collective-permute-done.3), channel_id=1, source_target_pairs={{0,48},{8,56},{16,0},{24,8},{32,16},{40,24},{48,32},{56,40},{64,11... | collective-permute-start | bytes 393224 | tf_op jit(solution)/shard_map/ppermute | solution.py:33
  18.5 6.2 %collective-permute-start.4 = (bf16[256,256]{1,0:T(8,128)(2,1)S(1)}, bf16[256,256]{1,0:T(8,128)(2,1)S(1)}, u32[]{:S(2)}, u32[]{:S(2)}) collective-permute-start(bf16[256,256]{1,0:T(8,128)(2,1)S(1)} %collective-permute-done.3), channel_id=1, source_target_pairs={{0,16},{8,24},{16,32},{24,40},{32,48},{40,56},{48,0},{56,8},{64,80... | collective-permute-start | bytes 393224 | tf_op jit(solution)/shard_map/ppermute | solution.py:33
  24.7 24.1 %collective-permute-start.7 = (bf16[1024,256]{1,0:T(8,128)(2,1)S(1)}, bf16[1024,256]{1,0:T(8,128)(2,1)S(1)}, u32[]{:S(2)}, u32[]{:S(2)}) collective-permute-start(bf16[1024,256]{1,0:T(8,128)(2,1)S(1)} %pad_maximum_fusion), channel_id=1, source_target_pairs={{0,16},{8,24},{16,32},{24,40},{32,48},{40,56},{48,0},{56,8},{64,80... | collective-permute-start | bytes 1572872 | tf_op jit(solution)/shard_map/ppermute | solution.py:33
  24.8 25.9 %collective-permute-start.8 = (bf16[1024,256]{1,0:T(8,128)(2,1)S(1)}, bf16[1024,256]{1,0:T(8,128)(2,1)S(1)}, u32[]{:S(2)}, u32[]{:S(2)}) collective-permute-start(bf16[1024,256]{1,0:T(8,128)(2,1)S(1)} %pad_maximum_fusion), channel_id=1, source_target_pairs={{0,48},{8,56},{16,0},{24,8},{32,16},{40,24},{48,32},{56,40},{64,11... | collective-permute-start | bytes 1572872 | tf_op jit(solution)/shard_map/ppermute | solution.py:33
  28.1 22.6 %collective-permute-start.9 = (bf16[1024,256]{1,0:T(8,128)(2,1)S(1)}, bf16[1024,256]{1,0:T(8,128)(2,1)S(1)}, u32[]{:S(2)}, u32[]{:S(2)}) collective-permute-start(bf16[1024,256]{1,0:T(8,128)(2,1)S(1)} %pad_maximum_fusion), channel_id=1, source_target_pairs={{0,32},{8,40},{16,48},{24,56},{32,0},{40,8},{48,16},{56,24},{64,96... | collective-permute-start | bytes 1572872 | tf_op jit(solution)/shard_map/ppermute | solution.py:33
  28.1 22.6 %collective-permute-start.10 = (bf16[1024,256]{1,0:T(8,128)(2,1)S(1)}, bf16[1024,256]{1,0:T(8,128)(2,1)S(1)}, u32[]{:S(2)}, u32[]{:S(2)}) collective-permute-start(bf16[1024,256]{1,0:T(8,128)(2,1)S(1)} %pad_maximum_fusion.1), channel_id=1, source_target_pairs={{0,64},{8,72},{16,80},{24,88},{32,96},{40,104},{48,112},{56,120},{... | collective-permute-start | bytes 1572872 | tf_op jit(solution)/shard_map/ppermute | solution.py:33
  29.0 21.8 %collective-permute-start.11 = (bf16[1024,256]{1,0:T(8,128)(2,1)S(1)}, bf16[1024,256]{1,0:T(8,128)(2,1)}, u32[]{:S(2)}, u32[]{:S(2)}) collective-permute-start(bf16[1024,256]{1,0:T(8,128)(2,1)S(1)} %pad_maximum_fusion.1), channel_id=1, source_target_pairs={{0,192},{8,200},{16,208},{24,216},{32,224},{40,232},{48,240},{56,2... | collective-permute-start | bytes 1572872 | tf_op jit(solution)/shard_map/ppermute | solution.py:33
  48.8 10.8 %collective-permute-start.12 = (bf16[1024,256]{1,0:T(8,128)(2,1)S(1)}, bf16[1024,256]{1,0:T(8,128)(2,1)}, u32[]{:S(2)}, u32[]{:S(2)}) collective-permute-start(bf16[1024,256]{1,0:T(8,128)(2,1)S(1)} %pad_maximum_fusion.1), channel_id=1, source_target_pairs={{0,128},{8,136},{16,144},{24,152},{32,160},{40,168},{48,176},{56,1... | collective-permute-start | bytes 1572872 | tf_op jit(solution)/shard_map/ppermute | solution.py:33
  78.8 8.2 %collective-permute-start.14 = (bf16[256,256]{1,0:T(8,128)(2,1)S(1)}, bf16[256,256]{1,0:T(8,128)(2,1)S(1)}, u32[]{:S(2)}, u32[]{:S(2)}) collective-permute-start(bf16[256,256]{1,0:T(8,128)(2,1)S(1)} %get-tuple-element.35), channel_id=1, source_target_pairs={{0,2},{1,3},{2,4},{3,5},{4,6},{5,7},{6,0},{7,1},{8,10},{9,11},{10,... | collective-permute-start | bytes 393224 | tf_op jit(solution)/shard_map/ppermute | solution.py:54
  80.7 8.5 %collective-permute-start.15 = (bf16[256,256]{1,0:T(8,128)(2,1)S(1)}, bf16[256,256]{1,0:T(8,128)(2,1)S(1)}, u32[]{:S(2)}, u32[]{:S(2)}) collective-permute-start(bf16[256,256]{1,0:T(8,128)(2,1)S(1)} %get-tuple-element.34), channel_id=1, source_target_pairs={{0,6},{1,7},{2,0},{3,1},{4,2},{5,3},{6,4},{7,5},{8,14},{9,15},{10,... | collective-permute-start | bytes 393224 | tf_op jit(solution)/shard_map/ppermute | solution.py:54
  82.7 11.4 %collective-permute-start.16 = (bf16[256,256]{1,0:T(8,128)(2,1)S(1)}, bf16[256,256]{1,0:T(8,128)(2,1)S(1)}, u32[]{:S(2)}, u32[]{:S(2)}) collective-permute-start(bf16[256,256]{1,0:T(8,128)(2,1)S(1)} %get-tuple-element.33), channel_id=1, source_target_pairs={{0,4},{1,5},{2,6},{3,7},{4,0},{5,1},{6,2},{7,3},{8,12},{9,13},{10,... | collective-permute-start | bytes 393224 | tf_op jit(solution)/shard_map/ppermute | solution.py:54
  97.3 8.4 %collective-permute-start.17 = (bf16[256,256]{1,0:T(8,128)(2,1)}, bf16[256,256]{1,0:T(8,128)(2,1)S(1)}, u32[]{:S(2)}, u32[]{:S(2)}) collective-permute-start(bf16[256,256]{1,0:T(8,128)(2,1)} %get-tuple-element.13), channel_id=1, source_target_pairs={{0,2},{1,3},{2,4},{3,5},{4,6},{5,7},{6,0},{7,1},{8,10},{9,11},{10,... | collective-permute-start | bytes 393224 | tf_op jit(solution)/shard_map/ppermute | solution.py:54
  97.3 8.5 %collective-permute-start.18 = (bf16[256,256]{1,0:T(8,128)(2,1)}, bf16[256,256]{1,0:T(8,128)(2,1)S(1)}, u32[]{:S(2)}, u32[]{:S(2)}) collective-permute-start(bf16[256,256]{1,0:T(8,128)(2,1)} %get-tuple-element.13), channel_id=1, source_target_pairs={{0,6},{1,7},{2,0},{3,1},{4,2},{5,3},{6,4},{7,5},{8,14},{9,15},{10,... | collective-permute-start | bytes 393224 | tf_op jit(solution)/shard_map/ppermute | solution.py:54
  102.1 8.8 %collective-permute-start.19 = (bf16[256,256]{1,0:T(8,128)(2,1)}, bf16[256,256]{1,0:T(8,128)(2,1)S(1)}, u32[]{:S(2)}, u32[]{:S(2)}) collective-permute-start(bf16[256,256]{1,0:T(8,128)(2,1)} %get-tuple-element.13), channel_id=1, source_target_pairs={{0,4},{1,5},{2,6},{3,7},{4,0},{5,1},{6,2},{7,3},{8,12},{9,13},{10,... | collective-permute-start | bytes 393224 | tf_op jit(solution)/shard_map/ppermute | solution.py:54
  134.0 16.4 %collective-permute-start.29 = (bf16[1024,256]{1,0:T(8,128)(2,1)S(1)}, bf16[1024,256]{1,0:T(8,128)(2,1)S(1)}, u32[]{:S(2)}, u32[]{:S(2)}) collective-permute-start(bf16[1024,256]{1,0:T(8,128)(2,1)S(1)} %bitcast.49), channel_id=1, source_target_pairs={{0,32},{8,40},{16,48},{24,56},{32,0},{40,8},{48,16},{56,24},{64,96... | collective-permute-start | bytes 1572872 | tf_op jit(solution)/shard_map/ppermute | solution.py:33
  134.1 23.1 %collective-permute-start.28 = (bf16[1024,256]{1,0:T(8,128)(2,1)S(1)}, bf16[1024,256]{1,0:T(8,128)(2,1)S(1)}, u32[]{:S(2)}, u32[]{:S(2)}) collective-permute-start(bf16[1024,256]{1,0:T(8,128)(2,1)S(1)} %bitcast.48), channel_id=1, source_target_pairs={{0,48},{8,56},{16,0},{24,8},{32,16},{40,24},{48,32},{56,40},{64,11... | collective-permute-start | bytes 1572872 | tf_op jit(solution)/shard_map/ppermute | solution.py:33
  134.5 26.6 %collective-permute-start.27 = (bf16[1024,256]{1,0:T(8,128)(2,1)S(1)}, bf16[1024,256]{1,0:T(8,128)(2,1)S(1)}, u32[]{:S(2)}, u32[]{:S(2)}) collective-permute-start(bf16[1024,256]{1,0:T(8,128)(2,1)S(1)} %bitcast.47), channel_id=1, source_target_pairs={{0,16},{8,24},{16,32},{24,40},{32,48},{40,56},{48,0},{56,8},{64,80... | collective-permute-start | bytes 1572872 | tf_op jit(solution)/shard_map/ppermute | solution.py:33
  136.3 27.9 %collective-permute-start.23 = (bf16[1088,256]{1,0:T(8,128)(2,1)S(1)}, bf16[1088,256]{1,0:T(8,128)(2,1)S(1)}, u32[]{:S(2)}, u32[]{:S(2)}) collective-permute-start(bf16[1088,256]{1,0:T(8,128)(2,1)S(1)} %bitcast.41), channel_id=1, source_target_pairs={{0,128},{8,136},{16,144},{24,152},{32,160},{40,168},{48,176},{56,1... | collective-permute-start | bytes 1671176 | tf_op jit(solution)/shard_map/ppermute | solution.py:33
  136.4 28.5 %collective-permute-start.22 = (bf16[1088,256]{1,0:T(8,128)(2,1)S(1)}, bf16[1088,256]{1,0:T(8,128)(2,1)S(1)}, u32[]{:S(2)}, u32[]{:S(2)}) collective-permute-start(bf16[1088,256]{1,0:T(8,128)(2,1)S(1)} %bitcast.40), channel_id=1, source_target_pairs={{0,192},{8,200},{16,208},{24,216},{32,224},{40,232},{48,240},{56,2... | collective-permute-start | bytes 1671176 | tf_op jit(solution)/shard_map/ppermute | solution.py:33
  150.3 14.6 %collective-permute-start.21 = (bf16[1088,256]{1,0:T(8,128)(2,1)S(1)}, bf16[1088,256]{1,0:T(8,128)(2,1)S(1)}, u32[]{:S(2)}, u32[]{:S(2)}) collective-permute-start(bf16[1088,256]{1,0:T(8,128)(2,1)S(1)} %bitcast.39), channel_id=1, source_target_pairs={{0,64},{8,72},{16,80},{24,88},{32,96},{40,104},{48,112},{56,120},{... | collective-permute-start | bytes 1671176 | tf_op jit(solution)/shard_map/ppermute | solution.py:33
  161.5 8.6 %collective-permute-start.32 = (bf16[256,256]{1,0:T(8,128)(2,1)S(1)}, bf16[256,256]{1,0:T(8,128)(2,1)S(1)}, u32[]{:S(2)}, u32[]{:S(2)}) collective-permute-start(bf16[256,256]{1,0:T(8,128)(2,1)S(1)} %get-tuple-element.31), channel_id=1, source_target_pairs={{0,128},{8,136},{16,144},{24,152},{32,160},{40,168},{48,176},{56,1... | collective-permute-start | bytes 393224 | tf_op jit(solution)/shard_map/ppermute | solution.py:33
  161.6 9.9 %collective-permute-start.31 = (bf16[256,256]{1,0:T(8,128)(2,1)S(1)}, bf16[256,256]{1,0:T(8,128)(2,1)S(1)}, u32[]{:S(2)}, u32[]{:S(2)}) collective-permute-start(bf16[256,256]{1,0:T(8,128)(2,1)S(1)} %get-tuple-element.32), channel_id=1, source_target_pairs={{0,192},{8,200},{16,208},{24,216},{32,224},{40,232},{48,240},{56,2... | collective-permute-start | bytes 393224 | tf_op jit(solution)/shard_map/ppermute | solution.py:33
  164.2 7.3 %collective-permute-start.30 = (bf16[256,256]{1,0:T(8,128)(2,1)S(1)}, bf16[256,256]{1,0:T(8,128)(2,1)S(1)}, u32[]{:S(2)}, u32[]{:S(2)}) collective-permute-start(bf16[256,256]{1,0:T(8,128)(2,1)S(1)} %get-tuple-element.30), channel_id=1, source_target_pairs={{0,64},{8,72},{16,80},{24,88},{32,96},{40,104},{48,112},{56,120},{... | collective-permute-start | bytes 393224 | tf_op jit(solution)/shard_map/ppermute | solution.py:33
  165.3 8.6 %collective-permute-start.26 = (bf16[272,256]{1,0:T(8,128)(2,1)S(1)}, bf16[272,256]{1,0:T(8,128)(2,1)S(1)}, u32[]{:S(2)}, u32[]{:S(2)}) collective-permute-start(bf16[272,256]{1,0:T(8,128)(2,1)S(1)} %get-tuple-element.28), channel_id=1, source_target_pairs={{0,32},{8,40},{16,48},{24,56},{32,0},{40,8},{48,16},{56,24},{64,96... | collective-permute-start | bytes 417800 | tf_op jit(solution)/shard_map/ppermute | solution.py:33
  169.4 5.5 %collective-permute-start.25 = (bf16[272,256]{1,0:T(8,128)(2,1)S(1)}, bf16[272,256]{1,0:T(8,128)(2,1)S(1)}, u32[]{:S(2)}, u32[]{:S(2)}) collective-permute-start(bf16[272,256]{1,0:T(8,128)(2,1)S(1)} %get-tuple-element.29), channel_id=1, source_target_pairs={{0,48},{8,56},{16,0},{24,8},{32,16},{40,24},{48,32},{56,40},{64,11... | collective-permute-start | bytes 417800 | tf_op jit(solution)/shard_map/ppermute | solution.py:33
  170.0 6.6 %collective-permute-start.24 = (bf16[272,256]{1,0:T(8,128)(2,1)S(1)}, bf16[272,256]{1,0:T(8,128)(2,1)S(1)}, u32[]{:S(2)}, u32[]{:S(2)}) collective-permute-start(bf16[272,256]{1,0:T(8,128)(2,1)S(1)} %get-tuple-element.27), channel_id=1, source_target_pairs={{0,16},{8,24},{16,32},{24,40},{32,48},{40,56},{48,0},{56,8},{64,80... | collective-permute-start | bytes 417800 | tf_op jit(solution)/shard_map/ppermute | solution.py:33
  176.7 11.3 %collective-permute-start.33 = (bf16[264,256]{1,0:T(8,128)(2,1)S(1)}, bf16[264,256]{1,0:T(8,128)(2,1)S(1)}, u32[]{:S(2)}, u32[]{:S(2)}) collective-permute-start(bf16[264,256]{1,0:T(8,128)(2,1)S(1)} %pad_maximum_fusion.2), channel_id=1, source_target_pairs={{0,8},{8,0},{16,24},{24,16},{32,40},{40,32},{48,56},{56,48},{64,72... | collective-permute-start | bytes 405512 | tf_op jit(solution)/shard_map/ppermute | solution.py:33
  (19 other events, 200.8 us)

commit v3 on v2

--- a/solution.py
+++ b/solution.py
@@ -287,9 +287,13 @@
     firsts = [first[0]] + [shift_y(first[step], step) for step in SHIFTS]
     seconds = [second[0]] + [shift_x(second[step], step) for step in SHIFTS]
     first, second = total(firsts), total(seconds)
-    away = jnp.concatenate([first[rows_a:], second[rows_b:]]).astype(BF16)
-    keep = jnp.concatenate([first[:rows_a], second[:rows_b]])
-    return keep + flip_z(away).astype(F32)
+    away_grad = first[rows_a + TILE :].astype(BF16)
+    grad = first[TILE:rows_a] + flip_z(away_grad).astype(F32)
+    away = jnp.concatenate(
+        [first[rows_a : rows_a + TILE], second[rows_b:]]
+    ).astype(BF16)
+    keep = jnp.concatenate([first[:TILE], second[:rows_b]])
+    return keep + flip_z(away).astype(F32), grad
 
 
 def on_device(features, weight, degrees, cotangent, tile_cols, list_len, tiles):
@@ -341,11 +345,9 @@
     first, second = backward(
         tiles, table, scatter_cols, list_len, near_rows, far_rows, weight_part
     )
-    kept = scatter_rows(first, second)
-
-    sums = jnp.concatenate([kept[:TILE], kept[TILE + EXTRA :]])
+    sums, weight_rows = scatter_rows(first, second)
+
     grad_x = (sums * inv_root[:, None]).astype(BF16)
-    weight_rows = kept[TILE : TILE + EXTRA]
     weight_rows = weight_rows + flip_core(weight_rows)
     weight_rows = total([weight_rows] + [shift_run(weight_rows, step) for step in SHIFTS])
     node_total = node_rows * lax.axis_size("row") * lax.axis_size("rep")

time: 199 us -> 205 us (1.030)
  waiting for transfers between devices: 91.2 us -> 96.1 us
  starting transfers between devices: 56.5 us -> 53.8 us
  Pallas kernels: 35.9 us -> 38.2 us
    ppermute x26 -> x27, waiting for transfers between devices: 63.3 us -> 70.4 us  [row_shift(): return lax.ppermute(value, 'row', pairs)]
    ppermute x26 -> x27, starting transfers between devices: 45.5 us -> 40.9 us  [row_shift(): return lax.ppermute(value, 'row', pairs)]
  transfers between devices with their start and end apart: 38 -> 39, of which waited for: 23 -> 24; matrix products, arithmetic and copies ran while one was open for 3% -> 3% of each run, Pallas kernels for 0% -> 0%
where the time goes in v3:
time: 205 us; the launch traced here: 202 us
  waiting for transfers between devices  96.1 us (47%)
  starting transfers between devices  53.8 us (26%)
  Pallas kernels  38.2 us (19%)
  local copies, waits for them, and re-layouts  8 us (4%)
  other arithmetic  5.33 us (3%)
    ppermute x27, waiting for transfers between devices, row_shift(): return lax.ppermute(value, 'row', pairs)  70.4 us
    ppermute x27, starting transfers between devices, row_shift(): return lax.ppermute(value, 'row', pairs)  40.9 us
    ppermute x9, waiting for transfers between devices, shift_run(): return lax.ppermute(value, 'rep', pairs)  23.1 us
    pallas_call x1, Pallas kernels, backward(): pl.pallas_call(backward_kernel, name='backward_product', out_shape=(jax.S...  20.4 us
    pallas_call x1, Pallas kernels, forward(): pl.pallas_call(forward_kernel, name='forward_product', out_shape=jax.Shap...  15.5 us
    ppermute x9, starting transfers between devices, shift_run(): return lax.ppermute(value, 'rep', pairs)  12.7 us
  transfers between devices with their start and end apart: 39, of which 24 were waited for; matrix products, arithmetic and copies ran while one was open for 3% of the time, Pallas kernels for 0%

profile of v3, /device:TPU:6, one launch (start us, length us, event | category | flops | bytes accessed | tf_op | source)
XLA Modules:
  0.0 202.4 jit_solution(374206025128790793)
XLA Ops:
  2.3 7.3 %collective-permute-start.3 = (bf16[256,256]{1,0:T(8,128)(2,1)S(1)}, bf16[256,256]{1,0:T(8,128)(2,1)S(1)}, u32[]{:S(2)}, u32[]{:S(2)}) collective-permute-start(bf16[256,256]{1,0:T(8,128)(2,1)S(1)} %multiply_convert_fusion), channel_id=1, source_target_pairs={{0,8},{8,0},{16,24},{24,16},{32,40},{40,32},{48,56},{56,48},{64,72... | collective-permute-start | bytes 393224 | tf_op jit(solution)/shard_map/ppermute | solution.py:33
  11.0 3.2 %collective-permute-start = (bf16[256,256]{1,0:T(8,128)(2,1)S(1)}, bf16[256,256]{1,0:T(8,128)(2,1)S(1)}, u32[]{:S(2)}, u32[]{:S(2)}) collective-permute-start(bf16[256,256]{1,0:T(8,128)(2,1)S(1)} %multiply_convert_fusion), channel_id=1, source_target_pairs={{0,64},{8,72},{16,80},{24,88},{32,96},{40,104},{48,112},{56,120},{... | collective-permute-start | bytes 393224 | tf_op jit(solution)/shard_map/ppermute | solution.py:33
  14.3 3.2 %collective-permute-start.6 = (bf16[256,256]{1,0:T(8,128)(2,1)S(1)}, bf16[256,256]{1,0:T(8,128)(2,1)S(1)}, u32[]{:S(2)}, u32[]{:S(2)}) collective-permute-start(bf16[256,256]{1,0:T(8,128)(2,1)S(1)} %collective-permute-done.3), channel_id=1, source_target_pairs={{0,32},{8,40},{16,48},{24,56},{32,0},{40,8},{48,16},{56,24},{64,96... | collective-permute-start | bytes 393224 | tf_op jit(solution)/shard_map/ppermute | solution.py:33
  19.5 2.3 %collective-permute-done.6 = bf16[256,256]{1,0:T(8,128)(2,1)S(1)} collective-permute-done((bf16[256,256]{1,0:T(8,128)(2,1)S(1)}, bf16[256,256]{1,0:T(8,128)(2,1)S(1)}, u32[]{:S(2)}, u32[]{:S(2)}) %collective-permute-start.6) | collective-permute-done | bytes 131104 | tf_op jit(solution)/shard_map/ppermute | solution.py:33
  24.8 3.2 %collective-permute-start.8 = (bf16[1024,256]{1,0:T(8,128)(2,1)S(1)}, bf16[1024,256]{1,0:T(8,128)(2,1)S(1)}, u32[]{:S(2)}, u32[]{:S(2)}) collective-permute-start(bf16[1024,256]{1,0:T(8,128)(2,1)S(1)} %pad_maximum_fusion), channel_id=1, source_target_pairs={{0,48},{8,56},{16,0},{24,8},{32,16},{40,24},{48,32},{56,40},{64,11... | collective-permute-start | bytes 1572872 | tf_op jit(solution)/shard_map/ppermute | solution.py:33
  30.1 18.7 %collective-permute-done.7 = bf16[1024,256]{1,0:T(8,128)(2,1)S(1)} collective-permute-done((bf16[1024,256]{1,0:T(8,128)(2,1)S(1)}, bf16[1024,256]{1,0:T(8,128)(2,1)S(1)}, u32[]{:S(2)}, u32[]{:S(2)}) %collective-permute-start.7) | collective-permute-done | bytes 524320 | tf_op jit(solution)/shard_map/ppermute | solution.py:33
  50.7 8.9 %collective-permute-done.12 = bf16[1024,256]{1,0:T(8,128)(2,1)} collective-permute-done((bf16[1024,256]{1,0:T(8,128)(2,1)S(1)}, bf16[1024,256]{1,0:T(8,128)(2,1)}, u32[]{:S(2)}, u32[]{:S(2)}) %collective-permute-start.12) | collective-permute-done | bytes 524320 | tf_op jit(solution)/shard_map/ppermute | solution.py:33
  59.6 15.5 %forward_product.1 = bf16[16,128,256]{2,1,0:T(8,128)(2,1)} custom-call(s32[16]{0:T(128)} %multiply_add_fusion.2.lists, s32[256]{0:T(256)} %reshape.90.cols, s32[16]{0:T(128)} %lens.3, bf16[16,16,128,128]{3,2,1,0:T(8,128)(2,1)} %tiles.3, bf16[8,128,256]{2,1,0:T(8,128)(2,1)} %bitcast.35, bf16[8,128,256]{2,1,0:T(8,128)(2,1)} %bitcast.42, ...), custom_call_target="tpu_custom_call" | custom-call | flops 2147483648 | bytes 12582912 | tf_op jit(solution)/shard_map/forward_product/pallas_call | solution.py:131
  76.5 1.9 collective-permute-done.13
  80.6 2.4 %collective-permute-start.15 = (bf16[256,256]{1,0:T(8,128)(2,1)S(1)}, bf16[256,256]{1,0:T(8,128)(2,1)S(1)}, u32[]{:S(2)}, u32[]{:S(2)}) collective-permute-start(bf16[256,256]{1,0:T(8,128)(2,1)S(1)} %get-tuple-element.36), channel_id=1, source_target_pairs={{0,6},{1,7},{2,0},{3,1},{4,2},{5,3},{6,4},{7,5},{8,14},{9,15},{10,... | collective-permute-start | bytes 393224 | tf_op jit(solution)/shard_map/ppermute | solution.py:54
  83.0 4.4 %collective-permute-done.14.one = bf16[256,256]{1,0:T(8,128)(2,1)S(1)} collective-permute-done((bf16[256,256]{1,0:T(8,128)(2,1)S(1)}, bf16[256,256]{1,0:T(8,128)(2,1)S(1)}, u32[]{:S(2)}, u32[]{:S(2)}) %collective-permute-start.14) | collective-permute-done | bytes 131104 | tf_op jit(solution)/shard_map/ppermute | solution.py:54
  87.4 2.0 collective-permute-done.15.two
  89.4 4.7 %collective-permute-done.16.three = bf16[256,256]{1,0:T(8,128)(2,1)S(1)} collective-permute-done((bf16[256,256]{1,0:T(8,128)(2,1)S(1)}, bf16[256,256]{1,0:T(8,128)(2,1)S(1)}, u32[]{:S(2)}, u32[]{:S(2)}) %collective-permute-start.16) | collective-permute-done | bytes 131104 | tf_op jit(solution)/shard_map/ppermute | solution.py:54
  94.9 2.4 %dense_middle.1 = (bf16[256,256]{1,0:T(8,128)(2,1)}, bf16[256,256]{1,0:T(8,128)(2,1)}, f32[256,256]{1,0:T(8,128)}) custom-call(bf16[256,256]{1,0:T(8,128)(2,1)} %get-tuple-element.38.own, bf16[256,256]{1,0:T(8,128)(2,1)} %copy-done.9, bf16[256,256]{1,0:T(8,128)(2,1)} %copy-done.10, bf16[256,256]{1,0:T(8,128)(2,1)} %copy-done.11, f32[256,256]{1,0:T(8,128)} %mul.77.inv, ...), custom_call_target="tpu_custom_call" | custom-call | tf_op jit(solution)/shard_map/dense_middle/pallas_call | solution.py:179
  97.3 3.8 %collective-permute-start.18 = (bf16[256,256]{1,0:T(8,128)(2,1)}, bf16[256,256]{1,0:T(8,128)(2,1)S(1)}, u32[]{:S(2)}, u32[]{:S(2)}) collective-permute-start(bf16[256,256]{1,0:T(8,128)(2,1)} %get-tuple-element.13), channel_id=1, source_target_pairs={{0,6},{1,7},{2,0},{3,1},{4,2},{5,3},{6,4},{7,5},{8,14},{9,15},{10,... | collective-permute-start | bytes 393224 | tf_op jit(solution)/shard_map/ppermute | solution.py:54
  102.1 3.6 %collective-permute-done.17 = bf16[256,256]{1,0:T(8,128)(2,1)S(1)} collective-permute-done((bf16[256,256]{1,0:T(8,128)(2,1)}, bf16[256,256]{1,0:T(8,128)(2,1)S(1)}, u32[]{:S(2)}, u32[]{:S(2)}) %collective-permute-start.17) | collective-permute-done | bytes 131104 | tf_op jit(solution)/shard_map/ppermute | solution.py:54
  105.7 5.0 %collective-permute-done.19 = bf16[256,256]{1,0:T(8,128)(2,1)S(1)} collective-permute-done((bf16[256,256]{1,0:T(8,128)(2,1)}, bf16[256,256]{1,0:T(8,128)(2,1)S(1)}, u32[]{:S(2)}, u32[]{:S(2)}) %collective-permute-start.19) | collective-permute-done | bytes 131104 | tf_op jit(solution)/shard_map/ppermute | solution.py:54
  113.6 20.4 %backward_product.1 = (bf16[32,136,256]{2,1,0:T(8,128)(2,1)}, bf16[32,128,256]{2,1,0:T(8,128)(2,1)}) custom-call(s32[48]{0:T(128)} %pad_add_fusion.chunks, s32[256]{0:T(256)} %reshape.99.cols, s32[16]{0:T(128)} %lens.3, bf16[16,16,128,128]{3,2,1,0:T(8,128)(2,1)} %tiles.3, bf16[8,128,256]{2,1,0:T(8,128)(2,1)} %bitcast.38, bf16[8,128,256]{2,1,0:T(8,128)(2,1)} %bitcast.50, ...), custom_call_target="tpu_custom_call" | custom-call | flops 2147483648 | bytes 16777216 | tf_op jit(solution)/shard_map/backward_product/pallas_call | solution.py:242
  136.3 2.9 %collective-permute-start.21 = (bf16[1088,256]{1,0:T(8,128)(2,1)S(1)}, bf16[1088,256]{1,0:T(8,128)(2,1)S(1)}, u32[]{:S(2)}, u32[]{:S(2)}) collective-permute-start(bf16[1088,256]{1,0:T(8,128)(2,1)S(1)} %bitcast.39), channel_id=1, source_target_pairs={{0,64},{8,72},{16,80},{24,88},{32,96},{40,104},{48,112},{56,120},{... | collective-permute-start | bytes 1671176 | tf_op jit(solution)/shard_map/ppermute | solution.py:33
  140.7 12.2 %collective-permute-done.23 = bf16[1088,256]{1,0:T(8,128)(2,1)S(1)} collective-permute-done((bf16[1088,256]{1,0:T(8,128)(2,1)S(1)}, bf16[1088,256]{1,0:T(8,128)(2,1)S(1)}, u32[]{:S(2)}, u32[]{:S(2)}) %collective-permute-start.23) | collective-permute-done | bytes 557088 | tf_op jit(solution)/shard_map/ppermute | solution.py:33
  153.0 6.9 %collective-permute-done.22 = bf16[1088,256]{1,0:T(8,128)(2,1)S(1)} collective-permute-done((bf16[1088,256]{1,0:T(8,128)(2,1)S(1)}, bf16[1088,256]{1,0:T(8,128)(2,1)S(1)}, u32[]{:S(2)}, u32[]{:S(2)}) %collective-permute-start.22) | collective-permute-done | bytes 557088 | tf_op jit(solution)/shard_map/ppermute | solution.py:33
  162.3 2.0 collective-permute-start.24
  164.3 1.9 collective-permute-done.27
  166.5 3.7 %collective-permute-done.26 = bf16[272,256]{1,0:T(8,128)(2,1)S(1)} collective-permute-done((bf16[272,256]{1,0:T(8,128)(2,1)S(1)}, bf16[272,256]{1,0:T(8,128)(2,1)S(1)}, u32[]{:S(2)}, u32[]{:S(2)}) %collective-permute-start.26) | collective-permute-done | bytes 139296 | tf_op jit(solution)/shard_map/ppermute | solution.py:33
  170.2 2.3 %collective-permute-done.24 = bf16[272,256]{1,0:T(8,128)(2,1)S(1)} collective-permute-done((bf16[272,256]{1,0:T(8,128)(2,1)S(1)}, bf16[272,256]{1,0:T(8,128)(2,1)S(1)}, u32[]{:S(2)}, u32[]{:S(2)}) %collective-permute-start.24) | collective-permute-done | bytes 139296 | tf_op jit(solution)/shard_map/ppermute | solution.py:33
  172.6 3.6 %collective-permute-start.34 = (bf16[8,256]{1,0:T(8,128)(2,1)S(1)}, bf16[8,256]{1,0:T(8,128)(2,1)S(1)}, u32[]{:S(2)}, u32[]{:S(2)}) collective-permute-start(bf16[8,256]{1,0:T(8,128)(2,1)S(1)} %slice.152), channel_id=1, source_target_pairs={{0,8},{8,0},{16,24},{24,16},{32,40},{40,32},{48,56},{56,48},{64,72... | collective-permute-start | bytes 12296 | tf_op jit(solution)/shard_map/ppermute | solution.py:33
  176.2 2.6 %collective-permute-start.32 = (bf16[256,256]{1,0:T(8,128)(2,1)S(1)}, bf16[256,256]{1,0:T(8,128)(2,1)S(1)}, u32[]{:S(2)}, u32[]{:S(2)}) collective-permute-start(bf16[256,256]{1,0:T(8,128)(2,1)S(1)} %get-tuple-element.33), channel_id=1, source_target_pairs={{0,128},{8,136},{16,144},{24,152},{32,160},{40,168},{48,176},{56,1... | collective-permute-start | bytes 393224 | tf_op jit(solution)/shard_map/ppermute | solution.py:33
  180.1 1.9 collective-permute-start.30
  183.4 2.2 %collective-permute-done.31 = bf16[256,256]{1,0:T(8,128)(2,1)S(1)} collective-permute-done((bf16[256,256]{1,0:T(8,128)(2,1)S(1)}, bf16[256,256]{1,0:T(8,128)(2,1)S(1)}, u32[]{:S(2)}, u32[]{:S(2)}) %collective-permute-start.31) | collective-permute-done | bytes 131104 | tf_op jit(solution)/shard_map/ppermute | solution.py:33
  186.2 4.3 %collective-permute-start.37 = (f32[8,256]{1,0:T(8,128)S(1)}, f32[8,256]{1,0:T(8,128)S(1)}, u32[]{:S(2)}, u32[]{:S(2)}) collective-permute-start(f32[8,256]{1,0:T(8,128)S(1)} %add.269), channel_id=1, source_target_pairs={{0,6},{1,7},{2,0},{3,1},{4,2},{5,3},{6,4},{7,5},{8,14},{9,15},{10,... | collective-permute-start | bytes 24584 | tf_op jit(solution)/shard_map/ppermute | solution.py:54
  192.7 3.4 %collective-permute-done.36 = f32[8,256]{1,0:T(8,128)S(1)} collective-permute-done((f32[8,256]{1,0:T(8,128)S(1)}, f32[8,256]{1,0:T(8,128)S(1)}, u32[]{:S(2)}, u32[]{:S(2)}) %collective-permute-start.36) | collective-permute-done | bytes 8224 | tf_op jit(solution)/shard_map/ppermute | solution.py:54
  196.7 5.0 %collective-permute-done.33 = bf16[256,256]{1,0:T(8,128)(2,1)S(1)} collective-permute-done((bf16[256,256]{1,0:T(8,128)(2,1)S(1)}, bf16[256,256]{1,0:T(8,128)(2,1)S(1)}, u32[]{:S(2)}, u32[]{:S(2)}) %collective-permute-start.33) | collective-permute-done | bytes 131104 | tf_op jit(solution)/shard_map/ppermute | solution.py:33
  (112 shorter events, 33.9 us)
Async XLA Ops:
  2.3 11.9 %collective-permute-start.3 = (bf16[256,256]{1,0:T(8,128)(2,1)S(1)}, bf16[256,256]{1,0:T(8,128)(2,1)S(1)}, u32[]{:S(2)}, u32[]{:S(2)}) collective-permute-start(bf16[256,256]{1,0:T(8,128)(2,1)S(1)} %multiply_convert_fusion), channel_id=1, source_target_pairs={{0,8},{8,0},{16,24},{24,16},{32,40},{40,32},{48,56},{56,48},{64,72... | collective-permute-start | bytes 393224 | tf_op jit(solution)/shard_map/ppermute | solution.py:33
  9.6 8.9 %collective-permute-start.2 = (bf16[256,256]{1,0:T(8,128)(2,1)S(1)}, bf16[256,256]{1,0:T(8,128)(2,1)S(1)}, u32[]{:S(2)}, u32[]{:S(2)}) collective-permute-start(bf16[256,256]{1,0:T(8,128)(2,1)S(1)} %multiply_convert_fusion), channel_id=1, source_target_pairs={{0,128},{8,136},{16,144},{24,152},{32,160},{40,168},{48,176},{56,1... | collective-permute-start | bytes 393224 | tf_op jit(solution)/shard_map/ppermute | solution.py:33
  11.0 8.5 %collective-permute-start.1 = (bf16[256,256]{1,0:T(8,128)(2,1)S(1)}, bf16[256,256]{1,0:T(8,128)(2,1)S(1)}, u32[]{:S(2)}, u32[]{:S(2)}) collective-permute-start(bf16[256,256]{1,0:T(8,128)(2,1)S(1)} %multiply_convert_fusion), channel_id=1, source_target_pairs={{0,192},{8,200},{16,208},{24,216},{32,224},{40,232},{48,240},{56,2... | collective-permute-start | bytes 393224 | tf_op jit(solution)/shard_map/ppermute | solution.py:33
  11.0 8.5 %collective-permute-start = (bf16[256,256]{1,0:T(8,128)(2,1)S(1)}, bf16[256,256]{1,0:T(8,128)(2,1)S(1)}, u32[]{:S(2)}, u32[]{:S(2)}) collective-permute-start(bf16[256,256]{1,0:T(8,128)(2,1)S(1)} %multiply_convert_fusion), channel_id=1, source_target_pairs={{0,64},{8,72},{16,80},{24,88},{32,96},{40,104},{48,112},{56,120},{... | collective-permute-start | bytes 393224 | tf_op jit(solution)/shard_map/ppermute | solution.py:33
  14.3 7.6 %collective-permute-start.6 = (bf16[256,256]{1,0:T(8,128)(2,1)S(1)}, bf16[256,256]{1,0:T(8,128)(2,1)S(1)}, u32[]{:S(2)}, u32[]{:S(2)}) collective-permute-start(bf16[256,256]{1,0:T(8,128)(2,1)S(1)} %collective-permute-done.3), channel_id=1, source_target_pairs={{0,32},{8,40},{16,48},{24,56},{32,0},{40,8},{48,16},{56,24},{64,96... | collective-permute-start | bytes 393224 | tf_op jit(solution)/shard_map/ppermute | solution.py:33
  24.7 24.1 %collective-permute-start.7 = (bf16[1024,256]{1,0:T(8,128)(2,1)S(1)}, bf16[1024,256]{1,0:T(8,128)(2,1)S(1)}, u32[]{:S(2)}, u32[]{:S(2)}) collective-permute-start(bf16[1024,256]{1,0:T(8,128)(2,1)S(1)} %pad_maximum_fusion), channel_id=1, source_target_pairs={{0,16},{8,24},{16,32},{24,40},{32,48},{40,56},{48,0},{56,8},{64,80... | collective-permute-start | bytes 1572872 | tf_op jit(solution)/shard_map/ppermute | solution.py:33
  24.8 25.9 %collective-permute-start.8 = (bf16[1024,256]{1,0:T(8,128)(2,1)S(1)}, bf16[1024,256]{1,0:T(8,128)(2,1)S(1)}, u32[]{:S(2)}, u32[]{:S(2)}) collective-permute-start(bf16[1024,256]{1,0:T(8,128)(2,1)S(1)} %pad_maximum_fusion), channel_id=1, source_target_pairs={{0,48},{8,56},{16,0},{24,8},{32,16},{40,24},{48,32},{56,40},{64,11... | collective-permute-start | bytes 1572872 | tf_op jit(solution)/shard_map/ppermute | solution.py:33
  28.1 22.6 %collective-permute-start.9 = (bf16[1024,256]{1,0:T(8,128)(2,1)S(1)}, bf16[1024,256]{1,0:T(8,128)(2,1)S(1)}, u32[]{:S(2)}, u32[]{:S(2)}) collective-permute-start(bf16[1024,256]{1,0:T(8,128)(2,1)S(1)} %pad_maximum_fusion), channel_id=1, source_target_pairs={{0,32},{8,40},{16,48},{24,56},{32,0},{40,8},{48,16},{56,24},{64,96... | collective-permute-start | bytes 1572872 | tf_op jit(solution)/shard_map/ppermute | solution.py:33
  28.1 22.6 %collective-permute-start.10 = (bf16[1024,256]{1,0:T(8,128)(2,1)S(1)}, bf16[1024,256]{1,0:T(8,128)(2,1)S(1)}, u32[]{:S(2)}, u32[]{:S(2)}) collective-permute-start(bf16[1024,256]{1,0:T(8,128)(2,1)S(1)} %pad_maximum_fusion.1), channel_id=1, source_target_pairs={{0,64},{8,72},{16,80},{24,88},{32,96},{40,104},{48,112},{56,120},{... | collective-permute-start | bytes 1572872 | tf_op jit(solution)/shard_map/ppermute | solution.py:33
  29.0 21.8 %collective-permute-start.11 = (bf16[1024,256]{1,0:T(8,128)(2,1)S(1)}, bf16[1024,256]{1,0:T(8,128)(2,1)}, u32[]{:S(2)}, u32[]{:S(2)}) collective-permute-start(bf16[1024,256]{1,0:T(8,128)(2,1)S(1)} %pad_maximum_fusion.1), channel_id=1, source_target_pairs={{0,192},{8,200},{16,208},{24,216},{32,224},{40,232},{48,240},{56,2... | collective-permute-start | bytes 1572872 | tf_op jit(solution)/shard_map/ppermute | solution.py:33
  48.8 10.8 %collective-permute-start.12 = (bf16[1024,256]{1,0:T(8,128)(2,1)S(1)}, bf16[1024,256]{1,0:T(8,128)(2,1)}, u32[]{:S(2)}, u32[]{:S(2)}) collective-permute-start(bf16[1024,256]{1,0:T(8,128)(2,1)S(1)} %pad_maximum_fusion.1), channel_id=1, source_target_pairs={{0,128},{8,136},{16,144},{24,152},{32,160},{40,168},{48,176},{56,1... | collective-permute-start | bytes 1572872 | tf_op jit(solution)/shard_map/ppermute | solution.py:33
  79.2 8.2 %collective-permute-start.14 = (bf16[256,256]{1,0:T(8,128)(2,1)S(1)}, bf16[256,256]{1,0:T(8,128)(2,1)S(1)}, u32[]{:S(2)}, u32[]{:S(2)}) collective-permute-start(bf16[256,256]{1,0:T(8,128)(2,1)S(1)} %get-tuple-element.37), channel_id=1, source_target_pairs={{0,2},{1,3},{2,4},{3,5},{4,6},{5,7},{6,0},{7,1},{8,10},{9,11},{10,... | collective-permute-start | bytes 393224 | tf_op jit(solution)/shard_map/ppermute | solution.py:54
  80.6 8.7 %collective-permute-start.15 = (bf16[256,256]{1,0:T(8,128)(2,1)S(1)}, bf16[256,256]{1,0:T(8,128)(2,1)S(1)}, u32[]{:S(2)}, u32[]{:S(2)}) collective-permute-start(bf16[256,256]{1,0:T(8,128)(2,1)S(1)} %get-tuple-element.36), channel_id=1, source_target_pairs={{0,6},{1,7},{2,0},{3,1},{4,2},{5,3},{6,4},{7,5},{8,14},{9,15},{10,... | collective-permute-start | bytes 393224 | tf_op jit(solution)/shard_map/ppermute | solution.py:54
  83.0 11.0 %collective-permute-start.16 = (bf16[256,256]{1,0:T(8,128)(2,1)S(1)}, bf16[256,256]{1,0:T(8,128)(2,1)S(1)}, u32[]{:S(2)}, u32[]{:S(2)}) collective-permute-start(bf16[256,256]{1,0:T(8,128)(2,1)S(1)} %get-tuple-element.35), channel_id=1, source_target_pairs={{0,4},{1,5},{2,6},{3,7},{4,0},{5,1},{6,2},{7,3},{8,12},{9,13},{10,... | collective-permute-start | bytes 393224 | tf_op jit(solution)/shard_map/ppermute | solution.py:54
  97.3 8.4 %collective-permute-start.17 = (bf16[256,256]{1,0:T(8,128)(2,1)}, bf16[256,256]{1,0:T(8,128)(2,1)S(1)}, u32[]{:S(2)}, u32[]{:S(2)}) collective-permute-start(bf16[256,256]{1,0:T(8,128)(2,1)} %get-tuple-element.13), channel_id=1, source_target_pairs={{0,2},{1,3},{2,4},{3,5},{4,6},{5,7},{6,0},{7,1},{8,10},{9,11},{10,... | collective-permute-start | bytes 393224 | tf_op jit(solution)/shard_map/ppermute | solution.py:54
  97.3 8.5 %collective-permute-start.18 = (bf16[256,256]{1,0:T(8,128)(2,1)}, bf16[256,256]{1,0:T(8,128)(2,1)S(1)}, u32[]{:S(2)}, u32[]{:S(2)}) collective-permute-start(bf16[256,256]{1,0:T(8,128)(2,1)} %get-tuple-element.13), channel_id=1, source_target_pairs={{0,6},{1,7},{2,0},{3,1},{4,2},{5,3},{6,4},{7,5},{8,14},{9,15},{10,... | collective-permute-start | bytes 393224 | tf_op jit(solution)/shard_map/ppermute | solution.py:54
  102.0 8.7 %collective-permute-start.19 = (bf16[256,256]{1,0:T(8,128)(2,1)}, bf16[256,256]{1,0:T(8,128)(2,1)S(1)}, u32[]{:S(2)}, u32[]{:S(2)}) collective-permute-start(bf16[256,256]{1,0:T(8,128)(2,1)} %get-tuple-element.13), channel_id=1, source_target_pairs={{0,4},{1,5},{2,6},{3,7},{4,0},{5,1},{6,2},{7,3},{8,12},{9,13},{10,... | collective-permute-start | bytes 393224 | tf_op jit(solution)/shard_map/ppermute | solution.py:54
  135.8 17.2 %collective-permute-start.23 = (bf16[1088,256]{1,0:T(8,128)(2,1)S(1)}, bf16[1088,256]{1,0:T(8,128)(2,1)S(1)}, u32[]{:S(2)}, u32[]{:S(2)}) collective-permute-start(bf16[1088,256]{1,0:T(8,128)(2,1)S(1)} %bitcast.41), channel_id=1, source_target_pairs={{0,128},{8,136},{16,144},{24,152},{32,160},{40,168},{48,176},{56,1... | collective-permute-start | bytes 1671176 | tf_op jit(solution)/shard_map/ppermute | solution.py:33
  135.9 24.0 %collective-permute-start.22 = (bf16[1088,256]{1,0:T(8,128)(2,1)S(1)}, bf16[1088,256]{1,0:T(8,128)(2,1)S(1)}, u32[]{:S(2)}, u32[]{:S(2)}) collective-permute-start(bf16[1088,256]{1,0:T(8,128)(2,1)S(1)} %bitcast.40), channel_id=1, source_target_pairs={{0,192},{8,200},{16,208},{24,216},{32,224},{40,232},{48,240},{56,2... | collective-permute-start | bytes 1671176 | tf_op jit(solution)/shard_map/ppermute | solution.py:33
  136.3 25.3 %collective-permute-start.21 = (bf16[1088,256]{1,0:T(8,128)(2,1)S(1)}, bf16[1088,256]{1,0:T(8,128)(2,1)S(1)}, u32[]{:S(2)}, u32[]{:S(2)}) collective-permute-start(bf16[1088,256]{1,0:T(8,128)(2,1)S(1)} %bitcast.39), channel_id=1, source_target_pairs={{0,64},{8,72},{16,80},{24,88},{32,96},{40,104},{48,112},{56,120},{... | collective-permute-start | bytes 1671176 | tf_op jit(solution)/shard_map/ppermute | solution.py:33
  139.4 22.9 %collective-permute-start.29 = (bf16[1024,256]{1,0:T(8,128)(2,1)S(1)}, bf16[1024,256]{1,0:T(8,128)(2,1)S(1)}, u32[]{:S(2)}, u32[]{:S(2)}) collective-permute-start(bf16[1024,256]{1,0:T(8,128)(2,1)S(1)} %bitcast.49), channel_id=1, source_target_pairs={{0,32},{8,40},{16,48},{24,56},{32,0},{40,8},{48,16},{56,24},{64,96... | collective-permute-start | bytes 1572872 | tf_op jit(solution)/shard_map/ppermute | solution.py:33
  139.5 24.8 %collective-permute-start.28 = (bf16[1024,256]{1,0:T(8,128)(2,1)S(1)}, bf16[1024,256]{1,0:T(8,128)(2,1)S(1)}, u32[]{:S(2)}, u32[]{:S(2)}) collective-permute-start(bf16[1024,256]{1,0:T(8,128)(2,1)S(1)} %bitcast.48), channel_id=1, source_target_pairs={{0,48},{8,56},{16,0},{24,8},{32,16},{40,24},{48,32},{56,40},{64,11... | collective-permute-start | bytes 1572872 | tf_op jit(solution)/shard_map/ppermute | solution.py:33
  153.0 13.2 %collective-permute-start.27 = (bf16[1024,256]{1,0:T(8,128)(2,1)S(1)}, bf16[1024,256]{1,0:T(8,128)(2,1)S(1)}, u32[]{:S(2)}, u32[]{:S(2)}) collective-permute-start(bf16[1024,256]{1,0:T(8,128)(2,1)S(1)} %bitcast.47), channel_id=1, source_target_pairs={{0,16},{8,24},{16,32},{24,40},{32,48},{40,56},{48,0},{56,8},{64,80... | collective-permute-start | bytes 1572872 | tf_op jit(solution)/shard_map/ppermute | solution.py:33
  162.1 8.1 %collective-permute-start.26 = (bf16[272,256]{1,0:T(8,128)(2,1)S(1)}, bf16[272,256]{1,0:T(8,128)(2,1)S(1)}, u32[]{:S(2)}, u32[]{:S(2)}) collective-permute-start(bf16[272,256]{1,0:T(8,128)(2,1)S(1)} %get-tuple-element.30), channel_id=1, source_target_pairs={{0,32},{8,40},{16,48},{24,56},{32,0},{40,8},{48,16},{56,24},{64,96... | collective-permute-start | bytes 417800 | tf_op jit(solution)/shard_map/ppermute | solution.py:33
  162.2 8.0 %collective-permute-start.25 = (bf16[272,256]{1,0:T(8,128)(2,1)S(1)}, bf16[272,256]{1,0:T(8,128)(2,1)S(1)}, u32[]{:S(2)}, u32[]{:S(2)}) collective-permute-start(bf16[272,256]{1,0:T(8,128)(2,1)S(1)} %get-tuple-element.31), channel_id=1, source_target_pairs={{0,48},{8,56},{16,0},{24,8},{32,16},{40,24},{48,32},{56,40},{64,11... | collective-permute-start | bytes 417800 | tf_op jit(solution)/shard_map/ppermute | solution.py:33
  162.3 10.2 %collective-permute-start.24 = (bf16[272,256]{1,0:T(8,128)(2,1)S(1)}, bf16[272,256]{1,0:T(8,128)(2,1)S(1)}, u32[]{:S(2)}, u32[]{:S(2)}) collective-permute-start(bf16[272,256]{1,0:T(8,128)(2,1)S(1)} %get-tuple-element.29), channel_id=1, source_target_pairs={{0,16},{8,24},{16,32},{24,40},{32,48},{40,56},{48,0},{56,8},{64,80... | collective-permute-start | bytes 417800 | tf_op jit(solution)/shard_map/ppermute | solution.py:33
  172.6 9.4 %collective-permute-start.34 = (bf16[8,256]{1,0:T(8,128)(2,1)S(1)}, bf16[8,256]{1,0:T(8,128)(2,1)S(1)}, u32[]{:S(2)}, u32[]{:S(2)}) collective-permute-start(bf16[8,256]{1,0:T(8,128)(2,1)S(1)} %slice.152), channel_id=1, source_target_pairs={{0,8},{8,0},{16,24},{24,16},{32,40},{40,32},{48,56},{56,48},{64,72... | collective-permute-start | bytes 12296 | tf_op jit(solution)/shard_map/ppermute | solution.py:33
  176.2 7.2 %collective-permute-start.32 = (bf16[256,256]{1,0:T(8,128)(2,1)S(1)}, bf16[256,256]{1,0:T(8,128)(2,1)S(1)}, u32[]{:S(2)}, u32[]{:S(2)}) collective-permute-start(bf16[256,256]{1,0:T(8,128)(2,1)S(1)} %get-tuple-element.33), channel_id=1, source_target_pairs={{0,128},{8,136},{16,144},{24,152},{32,160},{40,168},{48,176},{56,1... | collective-permute-start | bytes 393224 | tf_op jit(solution)/shard_map/ppermute | solution.py:33
  178.8 6.8 %collective-permute-start.31 = (bf16[256,256]{1,0:T(8,128)(2,1)S(1)}, bf16[256,256]{1,0:T(8,128)(2,1)S(1)}, u32[]{:S(2)}, u32[]{:S(2)}) collective-permute-start(bf16[256,256]{1,0:T(8,128)(2,1)S(1)} %get-tuple-element.34), channel_id=1, source_target_pairs={{0,192},{8,200},{16,208},{24,216},{32,224},{40,232},{48,240},{56,2... | collective-permute-start | bytes 393224 | tf_op jit(solution)/shard_map/ppermute | solution.py:33
  186.1 6.4 %collective-permute-start.38 = (f32[8,256]{1,0:T(8,128)S(1)}, f32[8,256]{1,0:T(8,128)S(1)}, u32[]{:S(2)}, u32[]{:S(2)}) collective-permute-start(f32[8,256]{1,0:T(8,128)S(1)} %add.269), channel_id=1, source_target_pairs={{0,4},{1,5},{2,6},{3,7},{4,0},{5,1},{6,2},{7,3},{8,12},{9,13},{10,... | collective-permute-start | bytes 24584 | tf_op jit(solution)/shard_map/ppermute | solution.py:54
  186.2 6.4 %collective-permute-start.37 = (f32[8,256]{1,0:T(8,128)S(1)}, f32[8,256]{1,0:T(8,128)S(1)}, u32[]{:S(2)}, u32[]{:S(2)}) collective-permute-start(f32[8,256]{1,0:T(8,128)S(1)} %add.269), channel_id=1, source_target_pairs={{0,6},{1,7},{2,0},{3,1},{4,2},{5,3},{6,4},{7,5},{8,14},{9,15},{10,... | collective-permute-start | bytes 24584 | tf_op jit(solution)/shard_map/ppermute | solution.py:54
  191.1 10.6 %collective-permute-start.33 = (bf16[256,256]{1,0:T(8,128)(2,1)S(1)}, bf16[256,256]{1,0:T(8,128)(2,1)S(1)}, u32[]{:S(2)}, u32[]{:S(2)}) collective-permute-start(bf16[256,256]{1,0:T(8,128)(2,1)S(1)} %pad_maximum_fusion.2), channel_id=1, source_target_pairs={{0,8},{8,0},{16,24},{24,16},{32,40},{40,32},{48,56},{56,48},{64,72... | collective-permute-start | bytes 393224 | tf_op jit(solution)/shard_map/ppermute | solution.py:33
  (20 other events, 212.7 us)
